TPU v7x, 128 devices: a whole 4x4x4 slice. The times are simulated.
128 devices in a mesh: rep: 4 (over z_lo, core), shard: 32 (over x, y, z_hi).
Axes of the slice: x: 4, y: 4, z: 4 (z_hi: 2, z_lo: 2; z = z_hi * 2 + z_lo), core: 2. Of those that a mesh axis runs over, the one named last changes fastest.
Arguments:
- tokens: bfloat16 [2, 32, 256, 1024], P(None, 'shard', 'rep'), may hold values from -6 to 6
- out_cotangent: bfloat16 [2, 32, 256, 1024], P(None, 'shard', 'rep'), may hold values from -6 to 6
- encoded: bfloat16 [2, 32, 4, 512, 1024], P(None, 'shard', None, 'rep'), may hold values from -6 to 6
- segment_ids: int32 [2, 32, 256], P(None, 'shard'), may hold values from 0 to 3, never falling along the last dimension, each value on 1 to 128 neighbouring positions
- doc_block: int32 [2, 32, 4], P(None, 'shard'), may hold values from 0 to 3, each once within a row
- bucket_table: int32 [256], replicated, may hold values from 0 to 31, as said below
- self_gain: bfloat16 [1024], P('shard'), may hold values from 0.5 to 1.5
- query_weight: bfloat16 [1024, 1024], P('shard'), may hold values from -0.046875 to 0.046875
- key_weight: bfloat16 [1024, 512], P('shard'), may hold values from -0.1875 to 0.1875
- value_weight: bfloat16 [1024, 512], P('shard'), may hold values from -0.1875 to 0.1875
- out_weight: bfloat16 [1024, 1024], P('shard'), may hold values from -0.75 to 0.75
- bias_table: bfloat16 [32, 16], P('shard'), may hold values from -3 to 3
- cross_gain: bfloat16 [1024], P('shard'), may hold values from 0.5 to 1.5
- cross_query: bfloat16 [1024, 1024], P('shard'), may hold values from -0.046875 to 0.046875
- cross_key: bfloat16 [1024, 512], P('shard'), may hold values from -0.1875 to 0.1875
- cross_value: bfloat16 [1024, 512], P('shard'), may hold values from -0.1875 to 0.1875
- cross_out: bfloat16 [1024, 1024], P('shard'), may hold values from -0.75 to 0.75
- feed_gain: bfloat16 [1024], P('shard'), may hold values from 0.5 to 1.5
- gate_weight: bfloat16 [1024, 2816], P('shard'), may hold values from -0.1875 to 0.1875
- up_weight: bfloat16 [1024, 2816], P('shard'), may hold values from -0.1875 to 0.1875
- down_weight: bfloat16 [2816, 1024], P('shard'), may hold values from -0.109375 to 0.109375
Outputs:
- layer_out: bfloat16 [2, 32, 256, 1024], P(None, 'shard', 'rep')
- tokens_grad: float32 [2, 32, 256, 1024], P(None, 'shard', 'rep')
- encoded_grad: float32 [2, 32, 4, 512, 1024], P(None, 'shard', None, 'rep')
- self_gain_grad: float32 [1024], P('shard')
- query_grad: float32 [1024, 1024], P('shard')
- key_grad: float32 [1024, 512], P('shard')
- value_grad: float32 [1024, 512], P('shard')
- out_grad: float32 [1024, 1024], P('shard')
- bias_grad: float32 [32, 16], P('shard')
- cross_gain_grad: float32 [1024], P('shard')
- cross_query_grad: float32 [1024, 1024], P('shard')
- cross_key_grad: float32 [1024, 512], P('shard')
- cross_value_grad: float32 [1024, 512], P('shard')
- cross_out_grad: float32 [1024, 1024], P('shard')
- feed_gain_grad: float32 [1024], P('shard')
- gate_grad: float32 [1024, 2816], P('shard')
- up_grad: float32 [1024, 2816], P('shard')
- down_grad: float32 [2816, 1024], P('shard')
Inputs may be any that keep to these rules, and one draw needn't show every extreme that they name: `segment_ids`: along each sequence the ids never fall; all 4 ids occur, each document has 1 to 128 tokens and one has exactly 128. `doc_block`: the 4 documents of a sequence read distinct encoder blocks of that sequence. `bucket_table`: never falls with the distance, equals the distance below 16, and reaches 31 at the largest distance.
All inputs are finite; a program needn't handle non-finite values.
Results may differ from a plain program's by a relative error of at most 0.033.
Values may be sent and summed in bfloat16 or wider, within the bound.
A program may use at most 320 MiB of HBM per device.

v0:
```python
import jax
import jax.numpy as jnp
from jax import lax
from jax.sharding import PartitionSpec as P

D = 1024
HEADS = 16
HEAD_DIM = 64
KV_GROUPS = 8
ENC = 512


epsilon = 1e-06
neg_big = -1e30


def for_sending(value):
    return jax.tree.map(lambda a: a.astype(jnp.bfloat16) if a.dtype == jnp.float32 else a, value)


def matmul(left, right):
    return jnp.dot(left, right, preferred_element_type=jnp.float32)


def left_contract(left, right):
    return lax.dot_general(
        left, right, (((0,), (0,)), ((), ())), preferred_element_type=jnp.float32
    )


def right_contract(left, right):
    return lax.dot_general(
        left, right, (((1,), (1,)), ((), ())), preferred_element_type=jnp.float32
    )


def rms_scale(values, gain):
    power = jnp.mean(values * values, axis=-1, keepdims=True)
    return values * lax.rsqrt(power + epsilon) * gain


def gated(gate, up_part):
    return jax.nn.gelu(gate, approximate=True) * up_part


def split_queries(queries):
    return queries.reshape(queries.shape[0], KV_GROUPS, HEADS // KV_GROUPS, HEAD_DIM)


def split_keys(keys):
    return keys.reshape(-1, KV_GROUPS, HEAD_DIM)


def scores_of(queries, keys, extra, allowed):
    raw = jnp.einsum(
        "qgjd,kgd->gjqk",
        split_queries(queries),
        split_keys(keys),
        preferred_element_type=jnp.float32,
    )
    return jnp.where(allowed, raw + extra, neg_big)


def attend(queries, keys, values, extra, allowed):
    scores = scores_of(queries, keys, extra, allowed)
    top = jnp.max(scores, axis=-1, keepdims=True)
    total = top + jnp.log(jnp.sum(jnp.exp(scores - top), axis=-1, keepdims=True))
    probs = jnp.exp(scores - total).astype(jnp.bfloat16)
    mixed = jnp.einsum(
        "gjqk,kgd->qgjd", probs, split_keys(values), preferred_element_type=jnp.float32
    )
    return (mixed.reshape(queries.shape[0], HEADS * HEAD_DIM).astype(jnp.bfloat16), total)


def attend_back(queries, keys, values, extra, allowed, total, context_grad):
    scores = scores_of(queries, keys, extra, allowed)
    probs = jnp.exp(scores - total)
    grad_four = split_queries(context_grad)
    prob_grad = jnp.einsum(
        "qgjd,kgd->gjqk", grad_four, split_keys(values), preferred_element_type=jnp.float32
    )
    score_grad = (probs * (prob_grad - jnp.sum(probs * prob_grad, axis=-1, keepdims=True))).astype(
        jnp.bfloat16
    )
    query_part = jnp.einsum(
        "gjqk,kgd->qgjd", score_grad, split_keys(keys), preferred_element_type=jnp.float32
    )
    query_part = query_part.reshape(queries.shape[0], HEADS * HEAD_DIM).astype(jnp.bfloat16)
    key_part = jnp.einsum(
        "gjqk,qgjd->kgd", score_grad, split_queries(queries), preferred_element_type=jnp.float32
    )
    value_part = jnp.einsum(
        "gjqk,qgjd->kgd", probs.astype(jnp.bfloat16), grad_four, preferred_element_type=jnp.float32
    )
    width = KV_GROUPS * HEAD_DIM
    return (query_part, key_part.reshape(-1, width), value_part.reshape(-1, width), score_grad)


def reduce_shards(grads):
    return jax.tree.map(
        lambda part: part.astype(jnp.float32),
        lax.psum_scatter(for_sending(grads), "shard", scatter_dimension=0, tiled=True),
    )


def local(
    tokens,
    out_cotangent,
    encoded,
    segment_ids,
    doc_block,
    bucket_table,
    self_gain,
    query_weight,
    key_weight,
    value_weight,
    out_weight,
    bias_table,
    cross_gain,
    cross_query,
    cross_key,
    cross_value,
    cross_out,
    feed_gain,
    gate_weight,
    up_weight,
    down_weight,
):
    micro = tokens.shape[0]
    rows = tokens.shape[2]
    length = segment_ids.shape[2]
    docs = encoded.shape[2]
    enc_local = encoded.shape[3]
    width = KV_GROUPS * HEAD_DIM
    buckets = bias_table.shape[0] * lax.axis_size("shard")
    start = lax.axis_index("rep") * rows
    query_pos = start + jnp.arange(rows, dtype=jnp.int32)
    key_pos = jnp.arange(length, dtype=jnp.int32)
    distance = jnp.clip(query_pos[:, None] - key_pos[None, :], 0, length - 1)
    bucket_ids = jnp.take(bucket_table, distance)
    bucket_hot = (
        bucket_ids.reshape(1, -1) == jnp.arange(buckets, dtype=jnp.int32)[:, None]
    ).astype(jnp.bfloat16)
    causal = key_pos[None, :] <= query_pos[:, None]
    key_block = jnp.arange(docs * ENC, dtype=jnp.int32) // ENC
    doc_ids = jnp.arange(docs, dtype=jnp.int32)
    all_parts = (
        query_weight,
        key_weight,
        value_weight,
        out_weight,
        self_gain,
        bias_table,
        cross_query,
        cross_key,
        cross_value,
        cross_out,
        cross_gain,
        gate_weight,
        up_weight,
        down_weight,
        feed_gain,
    )

    def fetch_all():
        whole = (
            lax.all_gather(all_parts[0], "shard", axis=0, tiled=True),
            lax.all_gather(all_parts[1], "shard", axis=0, tiled=True),
            lax.all_gather(all_parts[2], "shard", axis=0, tiled=True),
            lax.all_gather(all_parts[3], "shard", axis=0, tiled=True),
            lax.all_gather(all_parts[4], "shard", axis=0, tiled=True),
            lax.all_gather(all_parts[5], "shard", axis=0, tiled=True),
            lax.all_gather(all_parts[6], "shard", axis=0, tiled=True),
            lax.all_gather(all_parts[7], "shard", axis=0, tiled=True),
            lax.all_gather(all_parts[8], "shard", axis=0, tiled=True),
            lax.all_gather(all_parts[9], "shard", axis=0, tiled=True),
            lax.all_gather(all_parts[10], "shard", axis=0, tiled=True),
            lax.all_gather(all_parts[11], "shard", axis=0, tiled=True),
            lax.all_gather(all_parts[12], "shard", axis=0, tiled=True),
            lax.all_gather(all_parts[13], "shard", axis=0, tiled=True),
            lax.all_gather(all_parts[14], "shard", axis=0, tiled=True),
        )
        return (whole[0:6], whole[6:11], whole[11:15])

    outputs = []
    token_grads = []
    encoder_grads = []
    for index in range(micro):
        forward_set = fetch_all()
        full_query, full_key, full_value, full_out, self_scale, full_table = forward_set[0]
        across_query, across_key, across_value, across_out, cross_scale = forward_set[1]
        full_gate, full_up, full_down, feed_scale = forward_set[2]
        self_factor = self_scale.astype(jnp.float32)
        cross_factor = cross_scale.astype(jnp.float32)
        feed_factor = feed_scale.astype(jnp.float32)
        token_float = tokens[index, 0].astype(jnp.float32)
        segments = segment_ids[index, 0]
        query_seg = lax.dynamic_slice_in_dim(segments, start, rows)
        self_allowed = causal & (query_seg[:, None] == segments[None, :])
        blocks = doc_block[index, 0]
        seq_block = jnp.sum(
            (segments[:, None] == doc_ids[None, :]).astype(jnp.int32) * blocks[None, :], axis=1
        )
        query_block = lax.dynamic_slice_in_dim(seq_block, start, rows)
        cross_allowed = query_block[:, None] == key_block[None, :]
        self_normed = rms_scale(token_float, self_factor).astype(jnp.bfloat16)
        queries = matmul(self_normed, full_query).astype(jnp.bfloat16)
        keys_own = matmul(self_normed, full_key).astype(jnp.bfloat16)
        values_own = matmul(self_normed, full_value).astype(jnp.bfloat16)
        keys, values = (
            lax.all_gather(keys_own, "rep", axis=0, tiled=True),
            lax.all_gather(values_own, "rep", axis=0, tiled=True),
        )
        extra = matmul(full_table.T, bucket_hot).reshape(
            KV_GROUPS, HEADS // KV_GROUPS, rows, length
        )
        context, self_total = attend(queries, keys, values, extra, self_allowed)
        hidden = token_float + matmul(context, full_out)
        cross_normed = rms_scale(hidden, cross_factor).astype(jnp.bfloat16)
        cross_queries = matmul(cross_normed, across_query).astype(jnp.bfloat16)
        encoder_rows = encoded[index, 0].reshape(-1, D)
        keys_enc = matmul(encoder_rows, across_key).astype(jnp.bfloat16)
        values_enc = matmul(encoder_rows, across_value).astype(jnp.bfloat16)
        gathered_k, gathered_v = (
            lax.all_gather(keys_enc.reshape(docs, enc_local, width), "rep", axis=1, tiled=True),
            lax.all_gather(values_enc.reshape(docs, enc_local, width), "rep", axis=1, tiled=True),
        )
        cross_keys = gathered_k.reshape(-1, width)
        cross_values = gathered_v.reshape(-1, width)
        cross_context, cross_total = attend(
            cross_queries, cross_keys, cross_values, 0.0, cross_allowed
        )
        hidden_two = hidden + matmul(cross_context, across_out)
        feed_normed = rms_scale(hidden_two, feed_factor).astype(jnp.bfloat16)
        gate = matmul(feed_normed, full_gate)
        up_part = matmul(feed_normed, full_up)
        inner = gated(gate, up_part).astype(jnp.bfloat16)
        result = hidden_two + matmul(inner, full_down)
        outputs.append(result.astype(jnp.bfloat16))
        back_set = fetch_all()
        full_query, full_key, full_value, full_out, self_scale, full_table = back_set[0]
        across_query, across_key, across_value, across_out, cross_scale = back_set[1]
        full_gate, full_up, full_down, feed_scale = back_set[2]
        grad_out = out_cotangent[index, 0].astype(jnp.float32)
        grad_low = grad_out.astype(jnp.bfloat16)
        down_acc = left_contract(inner, grad_low)
        inner_grad = right_contract(grad_low, full_down)
        unused_inner, gated_back = jax.vjp(gated, gate, up_part)
        gate_part, up_grad_part = gated_back(inner_grad)
        gate_low = gate_part.astype(jnp.bfloat16)
        up_low = up_grad_part.astype(jnp.bfloat16)
        gate_acc = left_contract(feed_normed, gate_low)
        up_acc = left_contract(feed_normed, up_low)
        normed_grad = right_contract(gate_low, full_gate) + right_contract(up_low, full_up)
        unused_norm, norm_back = jax.vjp(rms_scale, hidden_two, feed_factor)
        hidden_grad, feed_acc = norm_back(normed_grad)
        hidden_grad = hidden_grad + grad_out
        branch_low = hidden_grad.astype(jnp.bfloat16)
        cross_out_acc = left_contract(cross_context, branch_low)
        context_grad = right_contract(branch_low, across_out).astype(jnp.bfloat16)
        cq_grad, ck_whole, cv_whole, cross_score_grad = attend_back(
            cross_queries, cross_keys, cross_values, 0.0, cross_allowed, cross_total, context_grad
        )
        ck_grad, cv_grad = (
            lax.psum_scatter(
                ck_whole.reshape(docs, ENC, width).astype(jnp.bfloat16),
                "rep",
                scatter_dimension=1,
                tiled=True,
            ).astype(jnp.float32),
            lax.psum_scatter(
                cv_whole.reshape(docs, ENC, width).astype(jnp.bfloat16),
                "rep",
                scatter_dimension=1,
                tiled=True,
            ).astype(jnp.float32),
        )
        ck_low = ck_grad.astype(jnp.bfloat16).reshape(-1, width)
        cv_low = cv_grad.astype(jnp.bfloat16).reshape(-1, width)
        cross_key_acc = left_contract(encoder_rows, ck_low)
        cross_value_acc = left_contract(encoder_rows, cv_low)
        encoder_grad = right_contract(ck_low, across_key) + right_contract(cv_low, across_value)
        encoder_grads.append(encoder_grad.reshape(docs, enc_local, D))
        cross_query_acc = left_contract(cross_normed, cq_grad)
        normed_grad = right_contract(cq_grad, across_query)
        unused_norm, norm_back = jax.vjp(rms_scale, hidden, cross_factor)
        hidden_part, cross_acc = norm_back(normed_grad)
        hidden_grad = hidden_grad + hidden_part
        branch_low = hidden_grad.astype(jnp.bfloat16)
        out_acc = left_contract(context, branch_low)
        context_grad = right_contract(branch_low, full_out).astype(jnp.bfloat16)
        q_grad, k_whole, v_whole, score_grad = attend_back(
            queries, keys, values, extra, self_allowed, self_total, context_grad
        )
        table_acc = right_contract(score_grad.reshape(HEADS, -1), bucket_hot).T
        k_grad, v_grad = (
            lax.psum_scatter(
                k_whole.astype(jnp.bfloat16), "rep", scatter_dimension=0, tiled=True
            ).astype(jnp.float32),
            lax.psum_scatter(
                v_whole.astype(jnp.bfloat16), "rep", scatter_dimension=0, tiled=True
            ).astype(jnp.float32),
        )
        k_low = k_grad.astype(jnp.bfloat16)
        v_low = v_grad.astype(jnp.bfloat16)
        query_acc = left_contract(self_normed, q_grad)
        key_acc = left_contract(self_normed, k_low)
        value_acc = left_contract(self_normed, v_low)
        normed_grad = (
            right_contract(q_grad, full_query)
            + right_contract(k_low, full_key)
            + right_contract(v_low, full_value)
        )
        unused_norm, norm_back = jax.vjp(rms_scale, token_float, self_factor)
        token_part, self_acc = norm_back(normed_grad)
        token_grads.append(hidden_grad + token_part)
        micro_grads = (
            self_acc,
            query_acc,
            key_acc,
            value_acc,
            out_acc,
            table_acc,
            cross_acc,
            cross_query_acc,
            cross_key_acc,
            cross_value_acc,
            cross_out_acc,
            feed_acc,
            gate_acc,
            up_acc,
            down_acc,
        )
        if index == 0:
            summed = micro_grads
        else:
            summed = tuple((first + second for first, second in zip(summed, micro_grads)))
    owned_total = reduce_shards(summed)
    final = jax.tree.map(
        lambda part: part.astype(jnp.float32), lax.psum(for_sending(owned_total), "rep")
    )
    layer_out = jnp.stack(outputs)[:, None]
    tokens_grad = jnp.stack(token_grads)[:, None]
    encoded_grad = jnp.stack(encoder_grads)[:, None]
    return (
        layer_out,
        tokens_grad,
        encoded_grad,
        final[0],
        final[1],
        final[2],
        final[3],
        final[4],
        final[5],
        final[6],
        final[7],
        final[8],
        final[9],
        final[10],
        final[11],
        final[12],
        final[13],
        final[14],
    )


def solution(mesh):
    in_specs = (
        P(None, "shard", "rep", None),
        P(None, "shard", "rep", None),
        P(None, "shard", None, "rep", None),
        P(None, "shard", None),
        P(None, "shard", None),
        P(),
        P("shard"),
        P("shard", None),
        P("shard", None),
        P("shard", None),
        P("shard", None),
        P("shard", None),
        P("shard"),
        P("shard", None),
        P("shard", None),
        P("shard", None),
        P("shard", None),
        P("shard"),
        P("shard", None),
        P("shard", None),
        P("shard", None),
    )
    out_specs = (
        P(None, "shard", "rep", None),
        P(None, "shard", "rep", None),
        P(None, "shard", None, "rep", None),
        P("shard"),
        P("shard", None),
        P("shard", None),
        P("shard", None),
        P("shard", None),
        P("shard", None),
        P("shard"),
        P("shard", None),
        P("shard", None),
        P("shard", None),
        P("shard", None),
        P("shard"),
        P("shard", None),
        P("shard", None),
        P("shard", None),
    )
    return jax.shard_map(local, mesh=mesh, in_specs=in_specs, out_specs=out_specs, check_vma=False)
```

profile of v0, /device:TPU:1, one launch (start us, length us, event | category | flops | bytes accessed | tf_op | source)
XLA Modules:
  0.0 4051.9 jit_solution(10622661398853307479)
XLA Ops:
  13.8 66.0 %all-gather.29.cloned.1.call-done = bf16[1024,512]{1,0:T(8,128)(2,1)} async-done(((bf16[32,512]{1,0:T(8,128)(2,1)}), bf16[1024,512]{1,0:T(8,128)(2,1)}) %all-gather.29.cloned.1.call-update) | async-done | bytes 1048592 | tf_op jit(solution)/shard_map/all_gather | solution.py:174
  82.7 64.1 %all-gather.25.cloned.1.call-done = bf16[1024,512]{1,0:T(8,128)(2,1)} async-done(((bf16[32,512]{1,0:T(8,128)(2,1)}), bf16[1024,512]{1,0:T(8,128)(2,1)}) %all-gather.25.cloned.1.call-update) | async-done | bytes 1048592 | tf_op jit(solution)/shard_map/all_gather | solution.py:175
  159.5 78.6 %all-reduce.8 = (bf16[1024]{0:T(1024)(128)(2,1)S(1)}, bf16[1024]{0:T(1024)(128)(2,1)S(1)}, bf16[1024]{0:T(1024)(128)(2,1)S(1)}) all-reduce(bf16[1024]{0:T(1024)(128)(2,1)S(1)} %dynamic-update-slice, bf16[1024]{0:T(1024)(128)(2,1)S(1)} %dynamic-update-slice.1, ...), channel_id=1, replica_groups=mesh['rep'=4,'shard'=32] {'shard'}, use_global_device_ids=true, to_apply=%add | all-reduce | flops 3072 | bytes 12288
  238.7 74.1 %all-gather = bf16[32,1,16]{2,1,0:T(2,128)(2,1)S(1)} all-gather(bf16[1,1,16]{2,1,0:T(2,128)(2,1)S(1)} %bitcast.699), channel_id=1, replica_groups=mesh['rep'=4,'shard'=32] {'shard'}, dimensions={0}, use_global_device_ids=true | all-gather | bytes 1056 | tf_op jit(solution)/shard_map/all_gather | solution.py:172
  313.0 101.9 %gather_fusion = s32[16384]{0:T(1024)S(1)} fusion(s32[256]{0:T(256)S(1)} %copy-done, s32[16384]{0:T(1024)S(1)} %broadcast_clamp_fusion), kind=kCustom, calls=%fused_computation | custom fusion | bytes 196608 | tf_op jit(solution)/shard_map/jit(_take)/gather | solution.py:140
  419.2 35.9 all_gather.48
  457.6 6.4 all_gather.126
  466.8 6.0 all_gather.125
  473.3 6.4 all_gather.50
  490.1 8.0 all-gather.33.cloned.1.call-done
  508.0 19.4 all-gather.45.cloned.1.call-done
  527.4 4.6 copy.140
  535.3 24.4 all-gather.43.cloned.1.call-done
  559.7 4.5 copy.139
  564.2 4.5 reshape.504
  568.7 22.6 all-gather.31.cloned.1.call-done
  591.3 4.5 copy.134
  600.2 22.8 all-gather.27.cloned.1.call-done
  623.0 4.5 copy.133
  627.5 4.5 reshape.500
  641.6 55.8 %all-gather.35.cloned.1.call-done = bf16[1024,1024]{1,0:T(8,128)(2,1)} async-done(((bf16[32,1024]{1,0:T(8,128)(2,1)}), bf16[1024,1024]{1,0:T(8,128)(2,1)}) %all-gather.35.cloned.1.call-update) | async-done | bytes 2097168 | tf_op jit(solution)/shard_map/all_gather | solution.py:176
  708.5 79.3 %all-gather.39.cloned.1.call-done = bf16[1024,2816]{1,0:T(8,128)(2,1)} async-done(((bf16[32,2816]{1,0:T(8,128)(2,1)}), bf16[1024,2816]{1,0:T(8,128)(2,1)}) %all-gather.39.cloned.1.call-update) | async-done | bytes 5767184 | tf_op jit(solution)/shard_map/all_gather | solution.py:179
  787.8 4.6 fusion.210
  792.4 85.5 %all-gather.37.cloned.1.call-done = bf16[1024,2816]{1,0:T(8,128)(2,1)} async-done(((bf16[32,2816]{1,0:T(8,128)(2,1)}), bf16[1024,2816]{1,0:T(8,128)(2,1)}) %all-gather.37.cloned.1.call-update) | async-done | bytes 5767184 | tf_op jit(solution)/shard_map/all_gather | solution.py:178
  877.9 4.6 fusion.209
  882.5 85.6 %all-gather.41.cloned.1.call-done = bf16[2816,1024]{1,0:T(8,128)(2,1)} async-done(((bf16[88,1024]{1,0:T(8,128)(2,1)}), bf16[2816,1024]{1,0:T(8,128)(2,1)}) %all-gather.41.cloned.1.call-update) | async-done | bytes 5767184 | tf_op jit(solution)/shard_map/all_gather | solution.py:180
  968.1 5.9 multiply_convert_fusion.3
  974.0 4.8 fusion.213
  978.8 5.3 multiply_reduce_fusion.3
  995.1 6.3 fusion.3
  1007.8 4.5 convert_element_type.560
  1012.3 46.3 %copy.182 = bf16[4,512,512]{0,2,1:T(8,128)(2,1)} copy(bf16[4,512,512]{1,0,2:T(4,128)(2,1)} %convert_element_type.560) | data formatting | bytes 4194304
  1058.6 128.6 %reshape.525 = bf16[512,2048]{1,0:T(8,128)(2,1)} reshape(bf16[512,512,4]{2,1,0:T(8,128)(2,1)} %bitcast.124) | data formatting | bytes 4194304
  1188.2 6.5 fusion
  1202.7 46.3 %copy.186 = bf16[4,512,512]{0,2,1:T(8,128)(2,1)} copy(bf16[4,512,512]{1,0,2:T(4,128)(2,1)} %convert_element_type.566) | data formatting | bytes 4194304
  1249.0 128.6 %reshape.529 = bf16[512,2048]{1,0:T(8,128)(2,1)} reshape(bf16[512,512,4]{2,1,0:T(8,128)(2,1)} %bitcast.130) | data formatting | bytes 4194304
  1377.7 6.9 fusion.13
  1387.9 46.1 %copy.188 = bf16[4,512,512]{0,2,1:T(8,128)(2,1)} copy(bf16[4,512,512]{1,0,2:T(4,128)(2,1)S(1)} %convert_element_type.569) | data formatting | bytes 4194304
  1434.0 128.6 %reshape.531 = bf16[512,2048]{1,0:T(8,128)(2,1)} reshape(bf16[512,512,4]{2,1,0:T(8,128)(2,1)} %bitcast.133) | data formatting | bytes 4194304
  1562.9 7.0 fusion.11
  1573.2 46.1 %copy.184 = bf16[4,512,512]{0,2,1:T(8,128)(2,1)} copy(bf16[4,512,512]{1,0,2:T(4,128)(2,1)S(1)} %convert_element_type.563) | data formatting | bytes 4194304
  1619.3 128.6 %reshape.527 = bf16[512,2048]{1,0:T(8,128)(2,1)} reshape(bf16[512,512,4]{2,1,0:T(8,128)(2,1)} %bitcast.127) | data formatting | bytes 4194304
  1748.0 5.1 fusion.52
  1784.6 37.9 reshape.526
  1822.5 15.9 copy.183
  1838.4 37.9 reshape.530
  1876.3 16.0 copy.187
  1899.5 37.9 reshape.532
  1937.4 15.9 copy.189
  1953.3 37.9 reshape.528
  1991.2 15.9 copy.185
  2074.6 153.1 %all-reduce.7 = (bf16[1024]{0:T(1024)(128)(2,1)S(1)}, bf16[32,16]{1,0:T(8,128)(2,1)S(1)}, bf16[1024]{0:T(1024)(128)(2,1)S(1)}, bf16[1024]{0:T(1024)(128)(2,1)S(1)}) all-reduce(bf16[1024]{0:T(1024)(128)(2,1)S(1)} %get-tuple-element.186, bf16[32,16]{1,0:T(8,128)(2,1)S(1)} %fusion.62, ...), channel_id=10, replica_groups=mesh['rep'=4,'shard'=32] {'shard'}, use_global_device_ids=true, to_apply=%region_36.37.clone | all-reduce | flops 3584 | bytes 14336
  2235.3 6.0 reduce-scatter.76.cloned.1.call-done
  2242.8 179.8 %reduce-scatter.42.cloned.1.call-done = bf16[32,512]{1,0:T(8,128)(2,1)} async-done(((bf16[1024,512]{1,0:T(8,128)(2,1)}), bf16[32,512]{1,0:T(8,128)(2,1)}) %reduce-scatter.42.cloned.1.call-update) | async-done | bytes 32784 | tf_op jit(solution)/shard_map/reduce_scatter | solution.py:102
  2422.6 181.0 %reduce-scatter.44.cloned.1.call-done = bf16[32,512]{1,0:T(8,128)(2,1)} async-done(((bf16[1024,512]{1,0:T(8,128)(2,1)}), bf16[32,512]{1,0:T(8,128)(2,1)}) %reduce-scatter.44.cloned.1.call-update) | async-done | bytes 32784 | tf_op jit(solution)/shard_map/reduce_scatter | solution.py:102
  2607.2 181.4 %reduce-scatter.50.cloned.1.call-done = bf16[32,1024]{1,0:T(8,128)(2,1)} async-done(((bf16[1024,1024]{1,0:T(8,128)(2,1)}), bf16[32,1024]{1,0:T(8,128)(2,1)}) %reduce-scatter.50.cloned.1.call-update) | async-done | bytes 65552 | tf_op jit(solution)/shard_map/reduce_scatter | solution.py:102
  2788.7 184.8 %reduce-scatter.48.cloned.1.call-done = bf16[32,1024]{1,0:T(8,128)(2,1)} async-done(((bf16[1024,1024]{1,0:T(8,128)(2,1)}), bf16[32,1024]{1,0:T(8,128)(2,1)}) %reduce-scatter.48.cloned.1.call-update) | async-done | bytes 65552 | tf_op jit(solution)/shard_map/reduce_scatter | solution.py:102
  2973.5 185.2 %reduce-scatter.46.cloned.1.call-done = bf16[32,1024]{1,0:T(8,128)(2,1)} async-done(((bf16[1024,1024]{1,0:T(8,128)(2,1)}), bf16[32,1024]{1,0:T(8,128)(2,1)}) %reduce-scatter.46.cloned.1.call-update) | async-done | bytes 65552 | tf_op jit(solution)/shard_map/reduce_scatter | solution.py:102
  3158.7 184.7 %reduce-scatter.40.cloned.1.call-done = bf16[32,1024]{1,0:T(8,128)(2,1)} async-done(((bf16[1024,1024]{1,0:T(8,128)(2,1)}), bf16[32,1024]{1,0:T(8,128)(2,1)}) %reduce-scatter.40.cloned.1.call-update) | async-done | bytes 65552 | tf_op jit(solution)/shard_map/reduce_scatter | solution.py:102
  3343.4 193.7 %reduce-scatter.54.cloned.1.call-done = bf16[32,2816]{1,0:T(8,128)(2,1)} async-done(((bf16[1024,2816]{1,0:T(8,128)(2,1)}), bf16[32,2816]{1,0:T(8,128)(2,1)}) %reduce-scatter.54.cloned.1.call-update) | async-done | bytes 180240 | tf_op jit(solution)/shard_map/reduce_scatter | solution.py:102
  3537.1 196.0 %reduce-scatter.52.cloned.1.call-done = bf16[32,2816]{1,0:T(8,128)(2,1)} async-done(((bf16[1024,2816]{1,0:T(8,128)(2,1)}), bf16[32,2816]{1,0:T(8,128)(2,1)}) %reduce-scatter.52.cloned.1.call-update) | async-done | bytes 180240 | tf_op jit(solution)/shard_map/reduce_scatter | solution.py:102
  3733.1 195.6 %reduce-scatter.56.cloned.1.call-done = bf16[88,1024]{1,0:T(8,128)(2,1)} async-done(((bf16[2816,1024]{1,0:T(8,128)(2,1)}), bf16[88,1024]{1,0:T(8,128)(2,1)}) %reduce-scatter.56.cloned.1.call-update) | async-done | bytes 180240 | tf_op jit(solution)/shard_map/reduce_scatter | solution.py:102
  3934.0 55.6 %all-reduce.14.cloned.1.call-done = (bf16[32,512]{0,1:T(8,128)(2,1)}, bf16[32,512]{0,1:T(8,128)(2,1)}, bf16[32]{0:T(256)(128)(2,1)}, bf16[32,512]{1,0:T(8,128)(2...) async-done(((bf16[32,512]{0,1:T(8,128)(2,1)}, bf16[32,512]{0,1:T(8,128)(2,1)}, bf16[32]{0:T(256)(128)(2,1)}, ...) | async-done | bytes 131312 | tf_op jit(solution)/shard_map/psum | solution.py:340
  4000.3 33.6 all-reduce.16.cloned.1.call-done
  (607 shorter events, 257.4 us)
Async XLA Ops:
  7.2 305.8 %copy-start = (s32[256]{0:T(256)S(1)}, s32[256]{0:T(256)}, u32[]{:S(2)}) copy-start(s32[256]{0:T(256)} %param.26) | copy-start | bytes 3076
  7.2 72.6 %all-gather.29.cloned.1.call-start = ((), (), s32[]{:S(2)}) async-start(), calls=%async_computation.25 | async-start | bytes 1081344 | tf_op jit(solution)/shard_map/all_gather | solution.py:174
  7.9 138.8 %all-gather.25.cloned.1.call-start = ((), (), s32[]{:S(2)}) async-start(), calls=%async_computation.23 | async-start | bytes 1081344 | tf_op jit(solution)/shard_map/all_gather | solution.py:175
  8.7 408.8 %all-gather.17.cloned.1.call-start = ((), (), s32[]{:S(2)}) async-start(), calls=%async_computation.19 | async-start | bytes 1081344 | tf_op jit(solution)/shard_map/all_gather | solution.py:169
  9.4 446.5 %all-gather.19.cloned.1.call-start = ((), (), s32[]{:S(2)}) async-start(), calls=%async_computation.20 | async-start | bytes 1081344 | tf_op jit(solution)/shard_map/all_gather | solution.py:168
  10.0 470.5 %all-gather.21.cloned.1.call-start = ((), (), s32[]{:S(2)}) async-start(), calls=%async_computation.21 | async-start | bytes 2162688 | tf_op jit(solution)/shard_map/all_gather | solution.py:167
  10.6 477.2 %all-gather.23.cloned.1.call-start = ((), (), s32[]{:S(2)}) async-start(), calls=%async_computation.22 | async-start | bytes 2162688 | tf_op jit(solution)/shard_map/all_gather | solution.py:170
  11.2 487.0 %all-gather.33.cloned.1.call-start = ((), (), s32[]{:S(2)}) async-start(), calls=%async_computation.27 | async-start | bytes 2162688 | tf_op jit(solution)/shard_map/all_gather | solution.py:173
  11.9 515.4 %all-gather.45.cloned.1.call-start = ((), (), s32[]{:S(2)}) async-start(), calls=%async_computation.33 | async-start | bytes 2621440 | tf_op jit(solution)/shard_map/all_gather | solution.py:225
  13.8 137.4 %copy-start.32 = (bf16[1,1,4,128,1024]{4,3,2,1,0:T(8,128)(2,1)}, bf16[1,1,4,128,1024]{4,3,2,1,0:T(8,128)(2,1)S(1)}, u32[]{:S(2)}) copy-start(bf16[1,1,4,128,1024]{4,3,2,1,0:T(8,128)(2,1)S(1)} %get-tuple-element.129) | copy-start | bytes 3145732
  13.8 137.5 %copy-start.25 = (bf16[1,1,4,128,1024]{4,3,2,1,0:T(8,128)(2,1)}, bf16[1,1,4,128,1024]{4,3,2,1,0:T(8,128)(2,1)S(1)}, u32[]{:S(2)}) copy-start(bf16[1,1,4,128,1024]{4,3,2,1,0:T(8,128)(2,1)S(1)} %get-tuple-element.128) | copy-start | bytes 3145732
  82.7 477.0 %all-gather.43.cloned.1.call-start = ((), (), s32[]{:S(2)}) async-start(), calls=%async_computation.32 | async-start | bytes 2621440 | tf_op jit(solution)/shard_map/all_gather | solution.py:226
  149.5 441.7 %all-gather.31.cloned.1.call-start = ((), (), s32[]{:S(2)}) async-start(), calls=%async_computation.26 | async-start | bytes 2621440 | tf_op jit(solution)/shard_map/all_gather | solution.py:225
  149.7 88.5 %copy-start.137 = (s32[2,1,256]{2,1,0:T(1,128)S(1)}, s32[2,1,256]{2,1,0:T(1,128)}, u32[]{:S(2)}) copy-start(s32[2,1,256]{2,1,0:T(1,128)} %param.24) | copy-start | bytes 6148
  149.7 89.0 %copy-start.147 = (bf16[1,16]{1,0:T(2,128)(2,1)S(1)}, bf16[1,16]{1,0:T(2,128)(2,1)}, u32[]{:S(2)}) copy-start(bf16[1,16]{1,0:T(2,128)(2,1)} %param.32) | copy-start | bytes 100
  151.2 471.8 %all-gather.27.cloned.1.call-start = ((), (), s32[]{:S(2)}) async-start(), calls=%async_computation.24 | async-start | bytes 2621440 | tf_op jit(solution)/shard_map/all_gather | solution.py:226
  154.1 543.4 %all-gather.35.cloned.1.call-start = ((), (), s32[]{:S(2)}) async-start(), calls=%async_computation.28 | async-start | bytes 2162688 | tf_op jit(solution)/shard_map/all_gather | solution.py:176
  154.6 633.1 %all-gather.39.cloned.1.call-start = ((), (), s32[]{:S(2)}) async-start(), calls=%async_computation.30 | async-start | bytes 5947392 | tf_op jit(solution)/shard_map/all_gather | solution.py:179
  155.4 722.5 %all-gather.37.cloned.1.call-start = ((), (), s32[]{:S(2)}) async-start(), calls=%async_computation.29 | async-start | bytes 5947392 | tf_op jit(solution)/shard_map/all_gather | solution.py:178
  156.0 812.1 %all-gather.41.cloned.1.call-start = ((), (), s32[]{:S(2)}) async-start(), calls=%async_computation.31 | async-start | bytes 5947392 | tf_op jit(solution)/shard_map/all_gather | solution.py:180
  156.6 1628.0 %reduce-scatter.66.cloned.1.call-start = ((), (), s32[]{:S(2)}) async-start(), calls=%async_computation.47 | async-start | bytes 2621440
  157.0 81.7 %copy-start.132 = (f32[64]{0:T(128)}, f32[64]{0:T(128)S(1)}, u32[]{:S(2)}) copy-start(f32[64]{0:T(128)S(1)} %get-tuple-element.104) | copy-start | bytes 772
  157.0 81.7 %copy-start.134 = (f32[64]{0:T(128)}, f32[64]{0:T(128)S(1)}, u32[]{:S(2)}) copy-start(f32[64]{0:T(128)S(1)} %get-tuple-element.105) | copy-start | bytes 772
  157.0 260.5 %copy-start.117 = (f32[64]{0:T(128)}, f32[64]{0:T(128)S(1)}, u32[]{:S(2)}) copy-start(f32[64]{0:T(128)S(1)} %fusion.181) | copy-start | bytes 772
  238.2 245.3 %copy-start.100 = (f32[1024]{0:T(1024)}, f32[1024]{0:T(1024)S(1)}, u32[]{:S(2)}) copy-start(f32[1024]{0:T(1024)S(1)} %convert_element_type.473) | copy-start | bytes 12292
  238.7 268.6 %copy-start.112 = (f32[1024]{0:T(1024)}, f32[1024]{0:T(1024)S(1)}, u32[]{:S(2)}) copy-start(f32[1024]{0:T(1024)S(1)} %convert_element_type.484) | copy-start | bytes 12292
  415.9 69.9 %copy-start.31 = (f32[2,8,64,256]{3,2,1,0:T(8,128)}, f32[2,8,64,256]{3,2,1,0:T(8,128)S(1)}, u32[]{:S(2)}) copy-start(f32[2,8,64,256]{3,2,1,0:T(8,128)S(1)} %copy.205) | copy-start | bytes 3145732
  490.1 217.1 %copy-start.27 = (f32[64,1024]{1,0:T(8,128)}, f32[64,1024]{1,0:T(8,128)S(1)}, u32[]{:S(2)}) copy-start(f32[64,1024]{1,0:T(8,128)S(1)} %get-tuple-element.158) | copy-start | bytes 786436
  506.7 190.7 %copy-start.29 = (f32[64,1024]{1,0:T(8,128)}, f32[64,1024]{1,0:T(8,128)S(1)}, u32[]{:S(2)}) copy-start(f32[64,1024]{1,0:T(8,128)S(1)} %get-tuple-element.164) | copy-start | bytes 786436
  508.0 124.1 %copy-start.63 = (bf16[64,1024]{0,1:T(8,128)(2,1)}, bf16[64,1024]{0,1:T(8,128)(2,1)S(1)}, u32[]{:S(2)}) copy-start(bf16[64,1024]{0,1:T(8,128)(2,1)S(1)} %copy.195) | copy-start | bytes 393220
  535.3 164.5 %copy-start.19 = (bf16[2048,8,64,1]{0,2,1,3:T(8,128)(2,1)}, bf16[2048,8,64,1]{0,2,1,3:T(8,128)(2,1)S(1)}, u32[]{:S(2)}) copy-start(bf16[2048,8,64,1]{0,2,1,3:T(8,128)(2,1)S(1)} %reshape.503) | copy-start | bytes 6291460
  699.7 293.8 %copy-start.41 = (f32[64,1024]{1,0:T(8,128)}, f32[64,1024]{1,0:T(8,128)S(1)}, u32[]{:S(2)}) copy-start(f32[64,1024]{1,0:T(8,128)S(1)} %get-tuple-element.168) | copy-start | bytes 786436
  707.1 85.3 %copy-start.98 = (bf16[8,64,2,64]{3,1,2,0:T(8,128)(2,1)}, bf16[8,64,2,64]{3,1,2,0:T(8,128)(2,1)S(1)}, u32[]{:S(2)}) copy-start(bf16[8,64,2,64]{3,1,2,0:T(8,128)(2,1)S(1)} %fusion.49) | copy-start | bytes 393220
  707.8 285.7 %copy-start.39 = (f32[64,1024]{1,0:T(8,128)}, f32[64,1024]{1,0:T(8,128)S(1)}, u32[]{:S(2)}) copy-start(f32[64,1024]{1,0:T(8,128)S(1)} %get-tuple-element.170) | copy-start | bytes 786436
  708.5 174.1 %copy-start.57 = (bf16[64,1024]{1,0:T(8,128)(2,1)}, bf16[64,1024]{1,0:T(8,128)(2,1)S(1)}, u32[]{:S(2)}) copy-start(bf16[64,1024]{1,0:T(8,128)(2,1)S(1)} %multiply_convert_fusion.8) | copy-start | bytes 393220
  994.1 193.2 %copy-start.54 = (f32[64,1024]{1,0:T(8,128)}, f32[64,1024]{1,0:T(8,128)S(1)}, u32[]{:S(2)}) copy-start(f32[64,1024]{1,0:T(8,128)S(1)} %get-tuple-element.139) | copy-start | bytes 786436
  1187.2 651.2 %reduce-scatter.70.cloned.1.call-start = ((), (), s32[]{:S(2)}) async-start(), calls=%async_computation.49 | async-start | bytes 2621440
  1377.6 521.9 %reduce-scatter.72.cloned.1.call-start = ((), (), s32[]{:S(2)}) async-start(), calls=%async_computation.50 | async-start | bytes 2621440
  1434.0 128.9 %copy-start.66 = (bf16[64,1024]{0,1:T(8,128)(2,1)S(1)}, bf16[64,1024]{0,1:T(8,128)(2,1)}, u32[]{:S(2)}) copy-start(bf16[64,1024]{0,1:T(8,128)(2,1)} %copy-done.65) | copy-start | bytes 393220
  1562.6 390.6 %reduce-scatter.68.cloned.1.call-start = ((), (), s32[]{:S(2)}) async-start(), calls=%async_computation.48 | async-start | bytes 2621440
  1747.9 266.2 %reduce-scatter.58.cloned.1.call-start = ((), (), s32[]{:S(2)}) async-start(), calls=%async_computation.43 | async-start | bytes 327680
  1771.7 245.1 %reduce-scatter.62.cloned.1.call-start = ((), (), s32[]{:S(2)}) async-start(), calls=%async_computation.45 | async-start | bytes 327680
  1778.4 241.7 %reduce-scatter.60.cloned.1.call-start = ((), (), s32[]{:S(2)}) async-start(), calls=%async_computation.44 | async-start | bytes 327680
  1782.3 240.6 %reduce-scatter.64.cloned.1.call-start = ((), (), s32[]{:S(2)}) async-start(), calls=%async_computation.46 | async-start | bytes 327680
  1784.5 449.2 %reduce-scatter.74.cloned.1.call-start = ((), (), s32[]{:S(2)}) async-start(), calls=%async_computation.51 | async-start | bytes 1081344
  1899.2 342.1 %reduce-scatter.76.cloned.1.call-start = ((), (), s32[]{:S(2)}) async-start(), calls=%async_computation.52 | async-start | bytes 1081344
  2014.0 408.6 %reduce-scatter.42.cloned.1.call-start = ((), (), s32[]{:S(2)}) async-start(), calls=%async_computation.35 | async-start | bytes 1081344 | tf_op jit(solution)/shard_map/reduce_scatter | solution.py:102
  2020.0 583.6 %reduce-scatter.44.cloned.1.call-start = ((), (), s32[]{:S(2)}) async-start(), calls=%async_computation.36 | async-start | bytes 1081344 | tf_op jit(solution)/shard_map/reduce_scatter | solution.py:102
  2026.1 762.6 %reduce-scatter.50.cloned.1.call-start = ((), (), s32[]{:S(2)}) async-start(), calls=%async_computation.39 | async-start | bytes 2162688 | tf_op jit(solution)/shard_map/reduce_scatter | solution.py:102
  2029.0 944.5 %reduce-scatter.48.cloned.1.call-start = ((), (), s32[]{:S(2)}) async-start(), calls=%async_computation.38 | async-start | bytes 2162688 | tf_op jit(solution)/shard_map/reduce_scatter | solution.py:102
  2032.1 1126.6 %reduce-scatter.46.cloned.1.call-start = ((), (), s32[]{:S(2)}) async-start(), calls=%async_computation.37 | async-start | bytes 2162688 | tf_op jit(solution)/shard_map/reduce_scatter | solution.py:102
  2035.2 1308.2 %reduce-scatter.40.cloned.1.call-start = ((), (), s32[]{:S(2)}) async-start(), calls=%async_computation.34 | async-start | bytes 2162688 | tf_op jit(solution)/shard_map/reduce_scatter | solution.py:102
  2039.3 1497.8 %reduce-scatter.54.cloned.1.call-start = ((), (), s32[]{:S(2)}) async-start(), calls=%async_computation.41 | async-start | bytes 5947392 | tf_op jit(solution)/shard_map/reduce_scatter | solution.py:102
  2045.2 1687.8 %reduce-scatter.52.cloned.1.call-start = ((), (), s32[]{:S(2)}) async-start(), calls=%async_computation.40 | async-start | bytes 5947392 | tf_op jit(solution)/shard_map/reduce_scatter | solution.py:102
  2052.2 1876.5 %reduce-scatter.56.cloned.1.call-start = ((), (), s32[]{:S(2)}) async-start(), calls=%async_computation.42 | async-start | bytes 5947392 | tf_op jit(solution)/shard_map/reduce_scatter | solution.py:102
  2060.0 1929.6 %all-reduce.14.cloned.1.call-start = ((), (), s32[]{:S(2)}) async-start(), calls=%async_computation.53 | async-start | bytes 659456 | tf_op jit(solution)/shard_map/psum | solution.py:340
  2072.4 158.2 %copy-start.133 = (f32[64]{0:T(128)S(1)}, f32[64]{0:T(128)}, u32[]{:S(2)}) copy-start(f32[64]{0:T(128)} %copy-done.132) | copy-start | bytes 772
  2072.4 158.2 %copy-start.135 = (f32[64]{0:T(128)S(1)}, f32[64]{0:T(128)}, u32[]{:S(2)}) copy-start(f32[64]{0:T(128)} %copy-done.134) | copy-start | bytes 772
  2072.8 158.8 %copy-start.45 = (bf16[4,128,512]{1,0,2:T(4,128)(2,1)S(1)}, bf16[4,128,512]{1,0,2:T(4,128)(2,1)}, u32[]{:S(2)}) copy-start(bf16[4,128,512]{1,0,2:T(4,128)(2,1)} %copy.187) | copy-start | bytes 1572868
  2233.7 1695.1 %copy-start.44 = (bf16[4,128,512]{1,0,2:T(4,128)(2,1)S(1)}, bf16[4,128,512]{1,0,2:T(4,128)(2,1)}, u32[]{:S(2)}) copy-start(bf16[4,128,512]{1,0,2:T(4,128)(2,1)} %copy.183) | copy-start | bytes 1572868
  2603.7 1327.2 %copy-start.46 = (bf16[4,128,512]{1,0,2:T(4,128)(2,1)S(1)}, bf16[4,128,512]{1,0,2:T(4,128)(2,1)}, u32[]{:S(2)}) copy-start(bf16[4,128,512]{1,0,2:T(4,128)(2,1)} %copy.185) | copy-start | bytes 1572868
  2603.7 1430.2 %all-reduce.16.cloned.1.call-start = ((), (), s32[]{:S(2)}) async-start(), calls=%async_computation.54 | async-start | bytes 1605632 | tf_op jit(solution)/shard_map/psum | solution.py:340
  2607.2 1323.6 %copy-start.51 = (bf16[1024,512]{1,0:T(8,128)(2,1)S(1)}, bf16[1024,512]{1,0:T(8,128)(2,1)}, u32[]{:S(2)}) copy-start(bf16[1024,512]{1,0:T(8,128)(2,1)} %all-gather.25.cloned.1.call-done) | copy-start | bytes 3145732
  3931.7 113.3 %copy-start.1 = (s32[256]{0:T(256)S(1)}, s32[256]{0:T(256)}, u32[]{:S(2)}) copy-start(s32[256]{0:T(256)} %param.26) | copy-start | bytes 3076
  (133 other events, 1001.7 us)
Sparse Core Ops, SparseCore 0:
  11.0 68.7 all-gather.28
  82.8 63.9 all-gather.24
  149.8 64.9 all-gather.16
  217.6 63.8 all-gather.18
  284.4 68.8 all-gather.20
  356.1 68.9 all-gather.22
  428.1 69.9 all-gather.32
  499.8 27.5 all-gather.44
  529.6 30.0 all-gather.42
  561.2 30.0 all-gather.30
  592.9 30.0 all-gather.26
  625.9 71.4 all-gather.34
  700.4 87.3 all-gather.38
  790.6 87.3 all-gather.36
  880.7 87.3 all-gather.40
  1187.3 26.6 reduce-scatter.65
  1377.7 26.4 reduce-scatter.69
  1562.8 26.3 reduce-scatter.71
  1748.0 26.4 reduce-scatter.67
  1776.8 18.4 reduce-scatter.57
  1797.8 18.2 reduce-scatter.61
  1818.5 18.1 reduce-scatter.59
  1839.2 18.2 reduce-scatter.63
  1899.3 158.7 reduce-scatter.73
  2060.6 180.6 reduce-scatter.75
  2243.5 179.0 reduce-scatter.41
  2424.9 178.6 reduce-scatter.43
  2606.0 182.6 reduce-scatter.49
  2791.2 182.2 reduce-scatter.47
  2975.7 182.9 reduce-scatter.45
  3161.2 182.1 reduce-scatter.39
  3345.8 191.2 reduce-scatter.53
  3539.3 193.6 reduce-scatter.51
  3735.5 193.1 reduce-scatter.55
  3932.9 56.6 all-reduce.13
  3992.5 41.3 all-reduce.15
where the time goes:
time: 4070 us; the launch traced here: 4050 us
  waiting for transfers between devices  2320 us (57%)
  local copies, waits for them, and re-layouts  1110 us (27%)
  blocking collectives  360 us (9%)
  matrix products  203 us (5%)
    reduce_scatter x9, waiting for transfers between devices, reduce_shards(): lax.psum_scatter(for_sending(grads), 'shard', scatter_dimension=0, tiled=...  1680 us
    unnamed x367, local copies, waits for them, and re-layouts  950 us
    unnamed x2, blocking collectives  232 us
    gather x1, local copies, waits for them, and re-layouts, local(): bucket_ids = jnp.take(bucket_table, distance)  102 us
    psum x2, waiting for transfers between devices, local(): lax.psum(for_sending(owned_total), 'rep')  89.2 us
    all_gather x1, waiting for transfers between devices, fetch_all(): lax.all_gather(all_parts[13], 'shard', axis=0, tiled=True)  85.6 us
    all_gather x1, waiting for transfers between devices, fetch_all(): lax.all_gather(all_parts[11], 'shard', axis=0, tiled=True)  85.5 us
  transfers between devices with their start and end apart: 36, of which 23 were waited for; matrix products, arithmetic and copies ran while one was open for 27% of the time, Pallas kernels for 0%

commit v1 on v0

v1 whole, which is shorter than its diff:
```python
import jax
import jax.numpy as jnp
from jax import lax
from jax.experimental import pallas as pl
from jax.experimental.pallas import tpu as pltpu
from jax.sharding import PartitionSpec as P

D = 1024
HEADS = 16
HEAD_DIM = 64
KV_GROUPS = 8
FF = 2816
BUCKETS = 32
ENC = 512
SEQ = 256
DOCS = 4
MICRO = 2

REP = 4
SHARDS = 32
ROWS = SEQ // REP
OWN_HEADS = HEADS // REP
OWN_GROUPS = KV_GROUPS // REP
QW = OWN_HEADS * HEAD_DIM
KW = OWN_GROUPS * HEAD_DIM
OWN_FF = FF // REP
WINDOW = 144

epsilon = 1e-06
neg_big = -1e30
f32 = jnp.float32
bf16 = jnp.bfloat16
vmem_limit = 40 * 1024 * 1024


def matmul(left, right):
    return jnp.dot(left, right, preferred_element_type=f32)


def left_contract(left, right):
    return lax.dot_general(left, right, (((0,), (0,)), ((), ())), preferred_element_type=f32)


def right_contract(left, right):
    return lax.dot_general(left, right, (((1,), (1,)), ((), ())), preferred_element_type=f32)


def skewed(row):
    n = row.shape[1]
    out = jnp.broadcast_to(row, (n, n))
    at = lax.broadcasted_iota(jnp.int32, (n, n), 0)
    step = 1
    while step < n:
        out = jnp.where((at & step) != 0, pltpu.roll(out, step, 1), out)
        step *= 2
    return out


def unskewed_sum(square):
    n = square.shape[1]
    at = lax.broadcasted_iota(jnp.int32, (n, n), 0)
    step = 1
    while step < n:
        square = jnp.where((at & step) != 0, pltpu.roll(square, n - step, 1), square)
        step *= 2
    return jnp.sum(square, axis=0, keepdims=True)


def softmax_parts(scores):
    top = jnp.max(scores, axis=-1, keepdims=True)
    raised = jnp.exp(scores - top)
    return raised * (1.0 / jnp.sum(raised, axis=-1, keepdims=True))


def self_mask(seg_col, seg_row):
    at_query = lax.broadcasted_iota(jnp.int32, (SEQ, SEQ), 0)
    at_key = lax.broadcasted_iota(jnp.int32, (SEQ, SEQ), 1)
    return (at_key <= at_query) & (seg_col == seg_row)


def fill_bias(curve_ref, bias_ref):
    for head in range(OWN_HEADS):
        bias_ref[head] = skewed(curve_ref[head : head + 1, :])


def self_forward_kernel(qkv_ref, seg_col_ref, seg_row_ref, curve_ref, out_ref, bias_ref):
    @pl.when(pl.program_id(0) == 0)
    def _():
        fill_bias(curve_ref, bias_ref)

    whole = qkv_ref[...].reshape(SEQ, QW + 2 * KW)
    allowed = self_mask(seg_col_ref[0], seg_row_ref[0])
    mixed = []
    for head in range(OWN_HEADS):
        group = head * OWN_GROUPS // OWN_HEADS
        query = whole[:, head * HEAD_DIM : (head + 1) * HEAD_DIM]
        key = whole[:, QW + group * HEAD_DIM : QW + (group + 1) * HEAD_DIM]
        value = whole[:, QW + KW + group * HEAD_DIM : QW + KW + (group + 1) * HEAD_DIM]
        scores = jnp.where(allowed, right_contract(query, key) + bias_ref[head], neg_big)
        probs = softmax_parts(scores).astype(bf16)
        mixed.append(matmul(probs, value))
    out_ref[...] = jnp.concatenate(mixed, axis=1).astype(bf16).reshape(out_ref.shape)


def self_backward_kernel(
    qkv_ref, grad_ref, seg_col_ref, seg_row_ref, curve_ref, out_ref, curve_grad_ref, bias_ref, sum_ref
):
    @pl.when(pl.program_id(0) == 0)
    def _():
        fill_bias(curve_ref, bias_ref)
        sum_ref[...] = jnp.zeros_like(sum_ref)

    whole = qkv_ref[...].reshape(SEQ, QW + 2 * KW)
    grads = grad_ref[...].reshape(SEQ, QW)
    allowed = self_mask(seg_col_ref[0], seg_row_ref[0])
    query_grads = []
    key_grads = [None] * OWN_GROUPS
    value_grads = [None] * OWN_GROUPS
    for head in range(OWN_HEADS):
        group = head * OWN_GROUPS // OWN_HEADS
        query = whole[:, head * HEAD_DIM : (head + 1) * HEAD_DIM]
        key = whole[:, QW + group * HEAD_DIM : QW + (group + 1) * HEAD_DIM]
        value = whole[:, QW + KW + group * HEAD_DIM : QW + KW + (group + 1) * HEAD_DIM]
        grad = grads[:, head * HEAD_DIM : (head + 1) * HEAD_DIM]
        scores = jnp.where(allowed, right_contract(query, key) + bias_ref[head], neg_big)
        probs = softmax_parts(scores)
        prob_grad = right_contract(grad, value)
        centred = prob_grad - jnp.sum(probs * prob_grad, axis=-1, keepdims=True)
        score_grad = (probs * centred).astype(bf16)
        sum_ref[head] += score_grad.astype(f32)
        query_grads.append(matmul(score_grad, key))
        key_part = left_contract(score_grad, query)
        value_part = left_contract(probs.astype(bf16), grad)
        if key_grads[group] is None:
            key_grads[group] = key_part
            value_grads[group] = value_part
        else:
            key_grads[group] = key_grads[group] + key_part
            value_grads[group] = value_grads[group] + value_part
    joined = jnp.concatenate(query_grads + key_grads + value_grads, axis=1)
    out_ref[...] = joined.astype(bf16).reshape(out_ref.shape)

    @pl.when(pl.program_id(0) == MICRO - 1)
    def _():
        curve_grad_ref[...] = jnp.zeros_like(curve_grad_ref)
        for head in range(OWN_HEADS):
            curve_grad_ref[head : head + 1, :] = unskewed_sum(sum_ref[head])


def cross_forward_kernel(block_ref, start_ref, q_ref, kv_ref, seg_ref, out_ref, query_ref, mixed_ref):
    at = pl.program_id(0) * DOCS + pl.program_id(1)

    @pl.when(pl.program_id(1) == 0)
    def _():
        query_ref[...] = q_ref[...].reshape(SEQ, QW)

    start = pl.multiple_of(start_ref[at], 16)
    rows = query_ref[pl.ds(start, WINDOW), :]
    mine = seg_ref[0, pl.ds(start, WINDOW), :] == pl.program_id(1)
    both = kv_ref[...].reshape(ENC, 2 * KW)
    mixed = []
    for head in range(OWN_HEADS):
        group = head * OWN_GROUPS // OWN_HEADS
        query = rows[:, head * HEAD_DIM : (head + 1) * HEAD_DIM]
        key = both[:, group * HEAD_DIM : (group + 1) * HEAD_DIM]
        value = both[:, KW + group * HEAD_DIM : KW + (group + 1) * HEAD_DIM]
        probs = softmax_parts(right_contract(query, key)).astype(bf16)
        mixed.append(matmul(probs, value))
    fresh = jnp.concatenate(mixed, axis=1)
    mixed_ref[pl.ds(start, WINDOW), :] = jnp.where(mine, fresh, mixed_ref[pl.ds(start, WINDOW), :])

    @pl.when(pl.program_id(1) == DOCS - 1)
    def _():
        out_ref[...] = mixed_ref[...].astype(bf16).reshape(out_ref.shape)


def cross_backward_kernel(
    block_ref, start_ref, q_ref, kv_ref, grad_ref, seg_ref, out_ref, kv_grad_ref, query_ref, given_ref, mixed_ref
):
    at = pl.program_id(0) * DOCS + pl.program_id(1)

    @pl.when(pl.program_id(1) == 0)
    def _():
        query_ref[...] = q_ref[...].reshape(SEQ, QW)
        given_ref[...] = grad_ref[...].reshape(SEQ, QW)

    start = pl.multiple_of(start_ref[at], 16)
    rows = query_ref[pl.ds(start, WINDOW), :]
    grads = given_ref[pl.ds(start, WINDOW), :]
    mine = seg_ref[0, pl.ds(start, WINDOW), :] == pl.program_id(1)
    both = kv_ref[...].reshape(ENC, 2 * KW)
    query_grads = []
    key_grads = [None] * OWN_GROUPS
    value_grads = [None] * OWN_GROUPS
    for head in range(OWN_HEADS):
        group = head * OWN_GROUPS // OWN_HEADS
        query = rows[:, head * HEAD_DIM : (head + 1) * HEAD_DIM]
        key = both[:, group * HEAD_DIM : (group + 1) * HEAD_DIM]
        value = both[:, KW + group * HEAD_DIM : KW + (group + 1) * HEAD_DIM]
        grad = grads[:, head * HEAD_DIM : (head + 1) * HEAD_DIM]
        probs = jnp.where(mine, softmax_parts(right_contract(query, key)), 0.0)
        prob_grad = right_contract(grad, value)
        centred = prob_grad - jnp.sum(probs * prob_grad, axis=-1, keepdims=True)
        score_grad = (probs * centred).astype(bf16)
        query_grads.append(matmul(score_grad, key))
        key_part = left_contract(score_grad, query)
        value_part = left_contract(probs.astype(bf16), grad)
        if key_grads[group] is None:
            key_grads[group] = key_part
            value_grads[group] = value_part
        else:
            key_grads[group] = key_grads[group] + key_part
            value_grads[group] = value_grads[group] + value_part
    fresh = jnp.concatenate(query_grads, axis=1)
    mixed_ref[pl.ds(start, WINDOW), :] = jnp.where(mine, fresh, mixed_ref[pl.ds(start, WINDOW), :])
    joined = jnp.concatenate(key_grads + value_grads, axis=1)
    kv_grad_ref[...] = joined.astype(bf16).reshape(kv_grad_ref.shape)

    @pl.when(pl.program_id(1) == DOCS - 1)
    def _():
        out_ref[...] = mixed_ref[...].astype(bf16).reshape(out_ref.shape)


def rows_block(width):
    return pl.BlockSpec((REP, 1, ROWS, width), lambda m, *rest: (0, m, 0, 0))


def fixed_block(shape):
    return pl.BlockSpec(shape, lambda *at: (0,) * len(shape))


def micro_block(shape):
    return pl.BlockSpec((1,) + shape, lambda m, *rest: (m,) + (0,) * len(shape))


def estimate(flops, moved, raised):
    return pl.CostEstimate(flops=flops, bytes_accessed=moved, transcendentals=raised)


self_pairs = MICRO * OWN_HEADS * SEQ * SEQ
cross_pairs = MICRO * OWN_HEADS * DOCS * WINDOW * ENC


def self_forward(qkv, seg_col, seg_row, curve):
    return pl.pallas_call(
        self_forward_kernel,
        name="self_forward",
        grid=(MICRO,),
        in_specs=[
            rows_block(QW + 2 * KW),
            micro_block((SEQ, 1)),
            micro_block((1, SEQ)),
            fixed_block((8, SEQ)),
        ],
        out_specs=rows_block(QW),
        out_shape=jax.ShapeDtypeStruct((REP, MICRO, ROWS, QW), bf16),
        scratch_shapes=[pltpu.VMEM((OWN_HEADS, SEQ, SEQ), f32)],
        compiler_params=pltpu.CompilerParams(vmem_limit_bytes=vmem_limit),
        cost_estimate=estimate(self_pairs * 256, 2 << 20, self_pairs),
    )(qkv, seg_col, seg_row, curve)


def self_backward(qkv, grads, seg_col, seg_row, curve):
    return pl.pallas_call(
        self_backward_kernel,
        name="self_backward",
        grid=(MICRO,),
        in_specs=[
            rows_block(QW + 2 * KW),
            rows_block(QW),
            micro_block((SEQ, 1)),
            micro_block((1, SEQ)),
            fixed_block((8, SEQ)),
        ],
        out_specs=[rows_block(QW + 2 * KW), fixed_block((8, SEQ))],
        out_shape=[
            jax.ShapeDtypeStruct((REP, MICRO, ROWS, QW + 2 * KW), bf16),
            jax.ShapeDtypeStruct((8, SEQ), f32),
        ],
        scratch_shapes=[
            pltpu.VMEM((OWN_HEADS, SEQ, SEQ), f32),
            pltpu.VMEM((OWN_HEADS, SEQ, SEQ), f32),
        ],
        compiler_params=pltpu.CompilerParams(vmem_limit_bytes=vmem_limit),
        cost_estimate=estimate(self_pairs * 640, 3 << 20, self_pairs),
    )(qkv, grads, seg_col, seg_row, curve)


def cross_rows():
    return pl.BlockSpec((REP, 1, ROWS, QW), lambda m, d, block, start: (0, m, 0, 0))


def cross_keys():
    return pl.BlockSpec(
        (REP, 1, 1, ENC // REP, 2 * KW),
        lambda m, d, block, start: (0, m, block[m * DOCS + d], 0, 0),
    )


def cross_segs():
    return pl.BlockSpec((1, SEQ, 1), lambda m, d, block, start: (m, 0, 0))


def cross_forward(blocks, starts, queries, kv, seg_col):
    return pl.pallas_call(
        cross_forward_kernel,
        name="cross_forward",
        grid_spec=pltpu.PrefetchScalarGridSpec(
            num_scalar_prefetch=2,
            grid=(MICRO, DOCS),
            in_specs=[cross_rows(), cross_keys(), cross_segs()],
            out_specs=cross_rows(),
            scratch_shapes=[pltpu.VMEM((SEQ, QW), bf16), pltpu.VMEM((SEQ, QW), f32)],
        ),
        out_shape=jax.ShapeDtypeStruct((REP, MICRO, ROWS, QW), bf16),
        compiler_params=pltpu.CompilerParams(vmem_limit_bytes=vmem_limit),
        cost_estimate=estimate(cross_pairs * 256, 3 << 20, cross_pairs),
    )(blocks, starts, queries, kv, seg_col)


def cross_backward(blocks, starts, queries, kv, grads, seg_col):
    return pl.pallas_call(
        cross_backward_kernel,
        name="cross_backward",
        grid_spec=pltpu.PrefetchScalarGridSpec(
            num_scalar_prefetch=2,
            grid=(MICRO, DOCS),
            in_specs=[cross_rows(), cross_keys(), cross_rows(), cross_segs()],
            out_specs=[cross_rows(), cross_keys()],
            scratch_shapes=[
                pltpu.VMEM((SEQ, QW), bf16),
                pltpu.VMEM((SEQ, QW), bf16),
                pltpu.VMEM((SEQ, QW), f32),
            ],
        ),
        out_shape=[
            jax.ShapeDtypeStruct((REP, MICRO, ROWS, QW), bf16),
            jax.ShapeDtypeStruct((REP, MICRO, DOCS, ENC // REP, 2 * KW), bf16),
        ],
        compiler_params=pltpu.CompilerParams(vmem_limit_bytes=vmem_limit),
        cost_estimate=estimate(cross_pairs * 640, 6 << 20, cross_pairs),
    )(blocks, starts, queries, kv, grads, seg_col)


swap_chip = [(i, i ^ 2) for i in range(REP)]
swap_core = [(i, i ^ 1) for i in range(REP)]
spread_rows = [
    (q * SHARDS + 8 * r + a, r * SHARDS + 4 * a + q)
    for q in range(REP)
    for r in range(REP)
    for a in range(SHARDS // REP)
]
collect_rows = [(there, here) for here, there in spread_rows]


def other_chip(value):
    return lax.ppermute(value, "rep", swap_chip)


def other_core(value):
    return lax.ppermute(value, "rep", swap_core)


def in_order(flag, own, other, axis):
    return jnp.where(flag == 0, jnp.stack([own, other], axis), jnp.stack([other, own], axis))


def gather_rep(value):
    rep = lax.axis_index("rep")
    pair = in_order(rep // 2, value, other_chip(value), 0)
    whole = in_order(rep % 2, pair, other_core(pair), 1)
    return whole.reshape((REP,) + value.shape)


def scatter_rep(parts):
    rep = lax.axis_index("rep")
    chip, core = rep // 2, rep % 2
    four = parts.reshape((2, 2) + parts.shape[1:])
    given = lax.dynamic_index_in_dim(four, 1 - core, 1, keepdims=False).astype(bf16)
    kept = lax.dynamic_index_in_dim(four, core, 1, keepdims=False)
    pair = kept + other_core(given).astype(f32)
    given = lax.dynamic_index_in_dim(pair, 1 - chip, 0, keepdims=False).astype(bf16)
    kept = lax.dynamic_index_in_dim(pair, chip, 0, keepdims=False)
    return kept + other_chip(given).astype(f32)


def gather_shard(block):
    return lax.all_to_all(
        jnp.broadcast_to(block[None], (SHARDS,) + block.shape), "shard", 0, 0, tiled=True
    )


def scatter_shard(parts):
    sent = lax.all_to_all(parts.astype(bf16), "shard", 0, 0, tiled=True)
    return jnp.sum(sent.astype(f32), axis=0)


def norm_parts(values):
    return lax.rsqrt(jnp.mean(values * values, axis=-1, keepdims=True) + epsilon)


def norm_backward(values, rho, gain, upstream):
    scaled = gain * upstream
    inner = jnp.mean(values * scaled, axis=-1, keepdims=True)
    back = rho * scaled - values * (rho * rho * rho * inner)
    return back, jnp.sum(values * rho * upstream, axis=0)


def local(
    tokens,
    out_cotangent,
    encoded,
    segment_ids,
    doc_block,
    bucket_table,
    self_gain,
    query_weight,
    key_weight,
    value_weight,
    out_weight,
    bias_table,
    cross_gain,
    cross_query,
    cross_key,
    cross_value,
    cross_out,
    feed_gain,
    gate_weight,
    up_weight,
    down_weight,
):
    rep = lax.axis_index("rep")
    own = MICRO * ROWS
    enc_rows = MICRO * DOCS * ENC // REP

    def columns(weight, width):
        return lax.dynamic_slice_in_dim(weight, rep * width, width, 1)

    def piece(weight, rows):
        return lax.dynamic_slice_in_dim(weight, rep * rows, rows, 0)

    qkv_block = jnp.concatenate(
        [columns(query_weight, QW), columns(key_weight, KW), columns(value_weight, KW)], axis=1
    )
    small = jnp.concatenate([self_gain, cross_gain, feed_gain, bias_table[0], jnp.zeros((16,), bf16)])
    small = jnp.broadcast_to(small[None], (8, 128))
    small = gather_shard(small)[:, 0]
    w_qkv = gather_shard(qkv_block).reshape(D, QW + 2 * KW)
    down_padded = jnp.pad(down_weight, ((0, 8), (0, 0)))
    rows_piece = jnp.concatenate([piece(out_weight, 8), piece(cross_out, 8), piece(down_padded, 24)], axis=0)
    rows_piece = lax.ppermute(rows_piece, ("rep", "shard"), spread_rows)
    ckv_block = jnp.stack(
        [cross_key.reshape(-1, REP, KW), cross_value.reshape(-1, REP, KW)], axis=2
    ).reshape(-1, 2 * REP * KW)
    w_ckv = gather_shard(ckv_block).reshape(D, 2 * REP * KW)
    w_out = gather_shard(rows_piece[0:8]).reshape(QW, D)
    w_cq = gather_shard(columns(cross_query, QW)).reshape(D, QW)
    w_cout = gather_shard(rows_piece[8:16]).reshape(QW, D)
    w_gate = gather_shard(columns(gate_weight, OWN_FF)).reshape(D, OWN_FF)
    w_up = gather_shard(columns(up_weight, OWN_FF)).reshape(D, OWN_FF)
    w_down = gather_shard(rows_piece[16:40]).reshape(8, 96, D)[:, :88].reshape(OWN_FF, D)
    self_factor = small[:, 0:32].reshape(D).astype(f32)
    cross_factor = small[:, 32:64].reshape(D).astype(f32)
    feed_factor = small[:, 64:96].reshape(D).astype(f32)
    table = small[:, 96:112]

    segments = segment_ids[:, 0]
    seg_col = segments[:, :, None]
    seg_row = segments[:, None, :]
    blocks = doc_block[:, 0].reshape(-1)
    doc_ids = jnp.arange(DOCS, dtype=jnp.int32)
    starts = jnp.sum((segments[:, None, :] < doc_ids[None, :, None]).astype(jnp.int32), axis=2)
    starts = jnp.minimum(starts // 16 * 16, SEQ - WINDOW).reshape(-1)
    turned = jnp.roll(bucket_table[::-1], 1)
    hot = (turned[None, :] == jnp.arange(BUCKETS, dtype=jnp.int32)[:, None]).astype(bf16)
    own_table = lax.dynamic_slice_in_dim(table, rep * OWN_HEADS, OWN_HEADS, 1)
    curve = left_contract(own_table, hot)
    curve = jnp.pad(curve, ((0, 4), (0, 0)))

    own_tokens = tokens.reshape(own, D)
    own_cotangent = out_cotangent.reshape(own, D)
    all_tokens = gather_rep(own_tokens).reshape(REP * own, D).astype(f32)
    all_grad = gather_rep(own_cotangent).reshape(REP * own, D)

    normed = (all_tokens * norm_parts(all_tokens) * self_factor).astype(bf16)
    qkv = matmul(normed, w_qkv).astype(bf16).reshape(REP, MICRO, ROWS, QW + 2 * KW)
    enc = encoded.reshape(enc_rows, D)
    ckv = jnp.stack(
        [matmul(enc, w_ckv[:, 2 * KW * r : 2 * KW * (r + 1)]).astype(bf16) for r in range(REP)]
    )
    kv = lax.all_to_all(ckv, "rep", 0, 0, tiled=True)
    kv = kv.reshape(REP, MICRO, DOCS, ENC // REP, 2 * KW)
    context = self_forward(qkv, seg_col, seg_row, curve).reshape(REP * own, QW)
    own_float = own_tokens.astype(f32)
    hidden = own_float + scatter_rep(matmul(context, w_out).reshape(REP, own, D))
    cross_rho = norm_parts(hidden)
    cross_normed = gather_rep((hidden * cross_rho * cross_factor).astype(bf16)).reshape(REP * own, D)
    cross_queries = matmul(cross_normed, w_cq).astype(bf16).reshape(REP, MICRO, ROWS, QW)
    cross_context = cross_forward(blocks, starts, cross_queries, kv, seg_col).reshape(REP * own, QW)
    hidden_two = hidden + scatter_rep(matmul(cross_context, w_cout).reshape(REP, own, D))
    feed_rho = norm_parts(hidden_two)
    feed_normed = gather_rep((hidden_two * feed_rho * feed_factor).astype(bf16)).reshape(REP * own, D)
    gate = matmul(feed_normed, w_gate)
    up_part = matmul(feed_normed, w_up)
    inner_grad = right_contract(all_grad, w_down)

    def gated(gate, up_part):
        return jax.nn.gelu(gate, approximate=True) * up_part

    inner, gated_back = jax.vjp(gated, gate, up_part)
    inner = inner.astype(bf16)
    gate_part, up_grad_part = gated_back(inner_grad)
    gate_low = gate_part.astype(bf16)
    up_low = up_grad_part.astype(bf16)

    own_grad = own_cotangent.astype(f32)
    feed_upstream = scatter_rep(
        (right_contract(gate_low, w_gate) + right_contract(up_low, w_up)).reshape(REP, own, D)
    )
    hidden_grad, feed_acc = norm_backward(hidden_two, feed_rho, feed_factor, feed_upstream)
    hidden_grad = hidden_grad + own_grad
    branch = gather_rep(hidden_grad.astype(bf16)).reshape(REP * own, D)
    layer_out = hidden_two + scatter_rep(matmul(inner, w_down).reshape(REP, own, D))
    gate_acc = scatter_shard(left_contract(feed_normed, gate_low).reshape(SHARDS, 32, OWN_FF))
    up_acc = scatter_shard(left_contract(feed_normed, up_low).reshape(SHARDS, 32, OWN_FF))
    down_part = left_contract(inner, all_grad).reshape(8, 88, D)
    down_part = jnp.pad(down_part.astype(bf16), ((0, 0), (0, 8), (0, 0)))
    down_acc = scatter_shard(down_part.reshape(SHARDS, 24, D))

    context_grad = right_contract(branch, w_cout).astype(bf16).reshape(REP, MICRO, ROWS, QW)
    cq_grad, kv_grad = cross_backward(blocks, starts, cross_queries, kv, context_grad, seg_col)
    cq_grad = cq_grad.reshape(REP * own, QW)
    cross_upstream = scatter_rep(right_contract(cq_grad, w_cq).reshape(REP, own, D))
    hidden_part, cross_acc = norm_backward(hidden, cross_rho, cross_factor, cross_upstream)
    hidden_grad = hidden_grad + hidden_part
    first_branch = gather_rep(hidden_grad.astype(bf16)).reshape(REP * own, D)
    cout_acc = scatter_shard(left_contract(cross_context, branch).reshape(SHARDS, 8, D))
    cq_acc = scatter_shard(left_contract(cross_normed, cq_grad).reshape(SHARDS, 32, QW))

    ckv_grad = lax.all_to_all(kv_grad.reshape(REP, enc_rows, 2 * KW), "rep", 0, 0, tiled=True)
    ckv_grad = jnp.concatenate([ckv_grad[r] for r in range(REP)], axis=1)
    encoder_grad = right_contract(ckv_grad, w_ckv)
    core = rep % 2
    half = REP * KW
    ckv_part = left_contract(enc, ckv_grad)
    given = lax.dynamic_slice_in_dim(ckv_part, (1 - core) * half, half, 1).astype(bf16)
    kept = lax.dynamic_slice_in_dim(ckv_part, core * half, half, 1)
    ckv_acc = scatter_shard((kept + other_core(given).astype(f32)).reshape(SHARDS, 32, half))

    context_grad = right_contract(first_branch, w_out).astype(bf16).reshape(REP, MICRO, ROWS, QW)
    qkv_grad, curve_grad = self_backward(qkv, context_grad, seg_col, seg_row, curve)
    qkv_grad = qkv_grad.reshape(REP * own, QW + 2 * KW)
    out_acc = scatter_shard(left_contract(context, first_branch).reshape(SHARDS, 8, D))
    qkv_acc = scatter_shard(left_contract(normed, qkv_grad).reshape(SHARDS, 32, QW + 2 * KW))
    self_upstream = scatter_rep(right_contract(qkv_grad, w_qkv).reshape(REP, own, D))
    self_rho = norm_parts(own_float)
    token_part, self_acc = norm_backward(own_float, self_rho, self_factor, self_upstream)
    tokens_grad = hidden_grad + token_part

    table_part = lax.dot_general(
        hot.astype(f32), curve_grad[:OWN_HEADS], (((1,), (1,)), ((), ())), precision=lax.Precision.HIGHEST
    )
    table_part = lax.dynamic_update_slice(jnp.zeros((BUCKETS, HEADS), f32), table_part, (0, rep * OWN_HEADS))
    small_part = jnp.concatenate(
        [
            self_acc.reshape(SHARDS, 32),
            cross_acc.reshape(SHARDS, 32),
            feed_acc.reshape(SHARDS, 32),
            table_part,
            jnp.zeros((SHARDS, 16), f32),
        ],
        axis=1,
    )
    small_sent = lax.all_to_all(
        jnp.broadcast_to(small_part[:, None], (SHARDS, 8, 128)), "shard", 0, 0, tiled=True
    )
    small_sum = jnp.sum(small_sent, axis=0)
    small_sum = small_sum + other_chip(small_sum)
    small_sum = (small_sum + other_core(small_sum))[0]

    def all_columns(value):
        whole = gather_rep(value.astype(bf16)).astype(f32)
        return jnp.concatenate([whole[r] for r in range(REP)], axis=1)

    rows_back = jnp.concatenate([out_acc, cout_acc, down_acc], axis=0).astype(bf16)
    rows_back = gather_rep(lax.ppermute(rows_back, ("rep", "shard"), collect_rows)).astype(f32)
    out_grad = rows_back[:, 0:8].reshape(32, D)
    cout_grad = rows_back[:, 8:16].reshape(32, D)
    down_grad = rows_back[:, 16:40].reshape(96, D)[:88]
    qkv_all = gather_rep(qkv_acc.astype(bf16)).astype(f32)
    query_grad = jnp.concatenate([qkv_all[r, :, :QW] for r in range(REP)], axis=1)
    key_grad = jnp.concatenate([qkv_all[r, :, QW : QW + KW] for r in range(REP)], axis=1)
    value_grad = jnp.concatenate([qkv_all[r, :, QW + KW :] for r in range(REP)], axis=1)
    cq_all = all_columns(cq_acc)
    gate_all = all_columns(gate_acc)
    up_all = all_columns(up_acc)
    ckv_acc = ckv_acc + other_chip(ckv_acc.astype(bf16)).astype(f32)
    ckv_acc = ckv_acc.astype(bf16)
    ckv_all = in_order(core, ckv_acc, other_core(ckv_acc), 1).astype(f32)
    ckv_all = ckv_all.reshape(32, REP, 2, KW)
    ck_grad = ckv_all[:, :, 0].reshape(32, REP * KW)
    cv_grad = ckv_all[:, :, 1].reshape(32, REP * KW)

    return (
        layer_out.astype(bf16).reshape(tokens.shape),
        tokens_grad.reshape(tokens.shape),
        encoder_grad.reshape(encoded.shape),
        small_sum[0:32],
        query_grad,
        key_grad,
        value_grad,
        out_grad,
        small_sum[96:112].reshape(1, HEADS),
        small_sum[32:64],
        cq_all,
        ck_grad,
        cv_grad,
        cout_grad,
        small_sum[64:96],
        gate_all,
        up_all,
        down_grad,
    )


def solution(mesh):
    rows = P("shard", None)
    gain = P("shard")
    acts = P(None, "shard", "rep", None)
    encs = P(None, "shard", None, "rep", None)
    ids = P(None, "shard", None)
    weights = (gain, rows, rows, rows, rows, rows, gain, rows, rows, rows, rows, gain, rows, rows, rows)
    return jax.shard_map(
        local,
        mesh=mesh,
        in_specs=(acts, acts, encs, ids, ids, P()) + weights,
        out_specs=(acts, acts, encs) + weights,
        check_vma=False,
    )
```

time: 4070 us -> 688 us (0.17)
  waiting for transfers between devices: 2320 us -> 219 us
  local copies, waits for them, and re-layouts: 1110 us -> 89.5 us
  blocking collectives: 360 us -> 0 us
  starting transfers between devices: 2.71 us -> 175 us
  matrix products: 203 us -> 60 us
  Pallas kernels: 0 us -> 52.3 us
    reduce_scatter x9 -> x0, waiting for transfers between devices: 1680 us -> none  [reduce_shards(): lax.psum_scatter(for_sending(grads), 'shard', scatter_dimension=0, tiled=...]
    unnamed x367 -> x141, local copies, waits for them, and re-layouts: 950 us -> 18.6 us
    all_gather x15 -> x0, waiting for transfers between devices: 533 us -> none  [the longest x1 85.6 us: fetch_all(): lax.all_gather(all_parts[13], 'shard', axis=0, tiled=True)]
    unnamed x2 -> x0, blocking collectives: 232 us -> none
    all_gather x5 -> x0, blocking collectives: 129 us -> none  [the longest x1 74.1 us: fetch_all(): lax.all_gather(all_parts[5], 'shard', axis=0, tiled=True)]
    all_to_all x0 -> x20, starting transfers between devices: none -> 127 us  [the longest x9 57.6 us: gather_shard(): lax.all_to_all(jnp.broadcast_to(block[None], (SHARDS,) + block.shape), 's...]
    all_to_all x0 -> x20, waiting for transfers between devices: none -> 111 us  [the longest x8 52.8 us: scatter_shard(): sent = lax.all_to_all(parts.astype(bf16), 'shard', 0, 0, tiled=True)]
    ppermute x0 -> x41, waiting for transfers between devices: none -> 108 us  [the longest x19 104 us: other_chip(): return lax.ppermute(value, 'rep', swap_chip)]
  transfers between devices with their start and end apart: 36 -> 61, of which waited for: 23 -> 31; matrix products, arithmetic and copies ran while one was open for 27% -> 29% of each run, Pallas kernels for 0% -> 8%
where the time goes in v1:
time: 688 us; the launch traced here: 676 us
  waiting for transfers between devices  219 us (32%)
  starting transfers between devices  175 us (25%)
  local copies, waits for them, and re-layouts  89.5 us (13%)
  other arithmetic  77.6 us (11%)
  matrix products  60 us (9%)
  Pallas kernels  52.3 us (8%)
    ppermute x19, waiting for transfers between devices, other_chip(): return lax.ppermute(value, 'rep', swap_chip)  104 us
    all_to_all x9, starting transfers between devices, gather_shard(): lax.all_to_all(jnp.broadcast_to(block[None], (SHARDS,) + block.shape), 's...  57.6 us
    all_to_all x8, waiting for transfers between devices, scatter_shard(): sent = lax.all_to_all(parts.astype(bf16), 'shard', 0, 0, tiled=True)  52.8 us
    all_to_all x9, waiting for transfers between devices, gather_shard(): lax.all_to_all(jnp.broadcast_to(block[None], (SHARDS,) + block.shape), 's...  49.2 us
    all_to_all x8, starting transfers between devices, scatter_shard(): sent = lax.all_to_all(parts.astype(bf16), 'shard', 0, 0, tiled=True)  48.1 us
    select_n x31, other arithmetic, in_order(): jnp.where(flag == 0, jnp.stack([own, other], axis), jnp.stack([other, own...  27.6 us
    ppermute x20, starting transfers between devices, other_core(): return lax.ppermute(value, 'rep', swap_core)  25 us
    dot_general x11, matrix products, matmul(): return jnp.dot(left, right, preferred_element_type=f32)  24.2 us
  transfers between devices with their start and end apart: 61, of which 31 were waited for; matrix products, arithmetic and copies ran while one was open for 29% of the time, Pallas kernels for 8%

profile of v1, /device:TPU:1, one launch (start us, length us, event | category | flops | bytes accessed | tf_op | source)
XLA Modules:
  0.0 675.8 jit_solution(9449198976205696500)
XLA Ops:
  2.4 6.9 %collective-permute-start.2 = (bf16[40,1024]{1,0:T(8,128)(2,1)S(1)}, bf16[40,1024]{1,0:T(8,128)(2,1)S(1)}, u32[]{:S(2)}, u32[]{:S(2)}) collective-permute-start(bf16[40,1024]{1,0:T(8,128)(2,1)S(1)} %pad_maximum_fusion.3), channel_id=1, source_target_pairs={{0,0},{1,4},{2,8},{3,12},{4,16},{5,20},{6,24},{7,28},{8,32},{9,36}... | collective-permute-start | bytes 245768 | tf_op jit(solution)/shard_map/ppermute | solution.py:451
  9.3 2.8 concatenate.206
  12.8 8.7 %all-to-all-start = ((bf16[32,8,128]{2,1,0:T(8,128)(2,1)}), bf16[32,8,128]{2,1,0:T(8,128)(2,1)S(1)}, u32[]{:S(2)}, u32[]{:S(2)}) async-start(bf16[32,8,128]{2,1,0:T(8,128)(2,1)} %broadcast_in_dim_broadcast_in_dim_broadcast_in_dim.2), calls=%async_computation | async-start | bytes 131072 | tf_op jit(solution)/shard_map/all_to_all | solution.py:388
  22.1 8.0 %all-to-all-done = bf16[32,8,128]{2,1,0:T(8,128)(2,1)S(1)} async-done(((bf16[32,8,128]{2,1,0:T(8,128)(2,1)}), bf16[32,8,128]{2,1,0:T(8,128)(2,1)S(1)}, u32[]{:S(2)}, u32[]{:S(2)}) %all-to-all-start) | async-done | bytes 65568 | tf_op jit(solution)/shard_map/all_to_all | solution.py:388
  31.0 3.9 all-to-all-start.2
  38.9 8.9 %all-to-all-done.2 = bf16[32,8,1024]{2,1,0:T(8,128)(2,1)S(1)} async-done(((bf16[32,8,1024]{2,1,0:T(8,128)(2,1)}), bf16[32,8,1024]{2,1,0:T(8,128)(2,1)S(1)}, u32[]{:S(2)}, u32[]{:S(2)}) %all-to-all-start.2) | async-done | bytes 524320 | tf_op jit(solution)/shard_map/all_to_all | solution.py:388
  49.7 4.7 all-to-all-start.1
  63.8 7.6 %all-to-all-done.1 = bf16[32,32,512]{2,1,0:T(8,128)(2,1)} async-done(((bf16[32,32,512]{2,1,0:T(8,128)(2,1)}), bf16[32,32,512]{2,1,0:T(8,128)(2,1)}, u32[]{:S(2)}, u32[]{:S(2)}) %all-to-all-start.1) | async-done | bytes 1048608 | tf_op jit(solution)/shard_map/all_to_all | solution.py:388
  73.0 4.8 all-to-all-start.4
  81.6 4.9 self_forward.1
  88.4 2.9 collective-permute-start.3
  96.1 8.6 %all-to-all-done.4 = bf16[32,32,1024]{2,1,0:T(8,128)(2,1)} async-done(((bf16[32,32,1024]{2,1,0:T(8,128)(2,1)}), bf16[32,32,1024]{2,1,0:T(8,128)(2,1)}, u32[]{:S(2)}, u32[]{:S(2)}) %all-to-all-start.4) | async-done | bytes 2097184 | tf_op jit(solution)/shard_map/all_to_all | solution.py:388
  105.6 6.4 all-to-all-start.3
  112.1 2.6 fusion.36
  114.7 2.6 fusion.35
  117.3 6.2 all-to-all-done.3
  124.4 4.8 all-to-all-start.6
  134.6 5.7 all-to-all-done.6
  140.3 8.6 %all-to-all-start.5 = ((bf16[4,1024,256]{1,2,0:T(8,128)(2,1)}), bf16[4,1024,256]{1,2,0:T(8,128)(2,1)}, u32[]{:S(2)}, u32[]{:S(2)}) async-start(bf16[4,1024,256]{1,2,0:T(8,128)(2,1)} %pad_maximum_fusion), calls=%async_computation.5 | async-start | bytes 4194304 | tf_op jit(solution)/shard_map/all_to_all | solution.py:491
  152.8 26.6 %collective-permute-done.5 = bf16[128,1024]{1,0:T(8,128)(2,1)} collective-permute-done((bf16[128,1024]{1,0:T(8,128)(2,1)}, bf16[128,1024]{1,0:T(8,128)(2,1)}, u32[]{:S(2)}, u32[]{:S(2)}) %collective-permute-start.5) | collective-permute-done | bytes 262176 | tf_op jit(solution)/shard_map/ppermute | solution.py:357
  186.7 4.7 all-to-all-start.7
  195.7 3.9 copy.190
  201.3 14.5 %cross_forward.1 = bf16[4,2,64,256]{3,2,1,0:T(8,128)(2,1)S(1)} custom-call(s32[8]{0:T(128)S(1)} %reshape_squeeze.9.block_ref, s32[8]{0:T(128)S(1)} %multiply_minimum_fusion.start_ref, bf16[4,2,64,256]{3,2,1,0:T(8,128)(2,1)S(1)} %bitcast.499, bf16[4,2,4,128,256]{4,3,2,1,0:T(8,128)(2,1)S(1)} %bitcast.488, ...), custom_call_target="tpu_custom_call" | custom-call | flops 603979776 | bytes 3145728 | tf_op jit(solution)/shard_map/cross_forward/pallas_call | solution.py:305
  220.8 9.6 %all-to-all-start.9 = ((bf16[32,24,1024]{2,1,0:T(8,128)(2,1)}), bf16[32,24,1024]{2,1,0:T(8,128)(2,1)}, u32[]{:S(2)}, u32[]{:S(2)}) async-start(bf16[32,24,1024]{2,1,0:T(8,128)(2,1)} %broadcast_in_dim.28), calls=%async_computation.9 | async-start | bytes 3145728 | tf_op jit(solution)/shard_map/all_to_all | solution.py:388
  235.4 19.0 %collective-permute-done.13 = bf16[128,1024]{1,0:T(8,128)(2,1)} collective-permute-done((bf16[128,1024]{1,0:T(8,128)(2,1)}, bf16[128,1024]{1,0:T(8,128)(2,1)}, u32[]{:S(2)}, u32[]{:S(2)}) %collective-permute-start.13) | collective-permute-done | bytes 262176 | tf_op jit(solution)/shard_map/ppermute | solution.py:357
  265.9 9.9 %all-to-all-start.8 = ((bf16[32,32,704]{2,1,0:T(8,128)(2,1)}), bf16[32,32,704]{2,1,0:T(8,128)(2,1)}, u32[]{:S(2)}, u32[]{:S(2)}) async-start(bf16[32,32,704]{2,1,0:T(8,128)(2,1)} %broadcast_in_dim.27), calls=%async_computation.8 | async-start | bytes 3145728 | tf_op jit(solution)/shard_map/all_to_all | solution.py:388
  290.8 3.9 fusion.94
  294.7 4.0 all-to-all-done.8
  298.7 4.4 fusion.32
  303.2 3.1 multiply_convert_fusion.1
  309.3 5.5 all-to-all-start.18
  327.6 2.8 dot_general.138
  330.4 3.6 convolution_convert_fusion
  334.0 3.3 all-to-all-done.18
  337.3 6.4 all-to-all-start.19
  343.8 2.7 fusion.41
  355.9 10.5 %all-to-all-done.19 = bf16[32,32,704]{2,1,0:T(8,128)(2,1)} async-done(((bf16[32,32,704]{2,1,0:T(8,128)(2,1)}), bf16[32,32,704]{2,1,0:T(8,128)(2,1)}, u32[]{:S(2)}, u32[]{:S(2)}) %all-to-all-start.19) | async-done | bytes 1441824 | tf_op jit(solution)/shard_map/all_to_all | solution.py:394
  366.5 5.2 all-to-all-start.15
  374.7 2.8 fusion.91
  387.1 9.7 %collective-permute-done.17 = bf16[128,1024]{1,0:T(8,128)(2,1)} collective-permute-done((bf16[128,1024]{1,0:T(8,128)(2,1)}, bf16[128,1024]{1,0:T(8,128)(2,1)}, u32[]{:S(2)}, u32[]{:S(2)}) %collective-permute-start.17) | collective-permute-done | bytes 262176 | tf_op jit(solution)/shard_map/ppermute | solution.py:357
  418.8 23.4 %cross_backward.1 = (bf16[4,2,64,256]{3,2,1,0:T(8,128)(2,1)S(1)}, bf16[4,2,4,128,256]{4,3,2,1,0:T(8,128)(2,1)S(1)}) custom-call(s32[8]{0:T(128)S(1)} %reshape_squeeze.9.block_ref, s32[8]{0:T(128)S(1)} %multiply_minimum_fusion.start_ref, bf16[4,2,64,256]{3,2,1,0:T(8,128)(2,1)S(1)} %bitcast.500, bf16[4,2,4,128,256]{4,3,2,1,0:T(8,128)(2,1)S(1)} %bitcast.489, ...), custom_call_target="tpu_custom_call" | custom-call | flops 1509949440 | bytes 6291456 | tf_op jit(solution)/shard_map/cross_backward/pallas_call | solution.py:322
  444.8 8.7 %all-to-all-start.16 = ((bf16[32,32,256]{2,1,0:T(8,128)(2,1)}), bf16[32,32,256]{2,1,0:T(8,128)(2,1)S(1)}, u32[]{:S(2)}, u32[]{:S(2)}) async-start(bf16[32,32,256]{2,1,0:T(8,128)(2,1)} %convolution_convert_fusion.4), calls=%async_computation.16 | async-start | bytes 1048576 | tf_op jit(solution)/shard_map/all_to_all | solution.py:394
  459.1 7.4 %all-to-all-done.16 = bf16[32,32,256]{2,1,0:T(8,128)(2,1)S(1)} async-done(((bf16[32,32,256]{2,1,0:T(8,128)(2,1)}), bf16[32,32,256]{2,1,0:T(8,128)(2,1)S(1)}, u32[]{:S(2)}, u32[]{:S(2)}) %all-to-all-start.16) | async-done | bytes 524320 | tf_op jit(solution)/shard_map/all_to_all | solution.py:394
  466.4 4.6 all-to-all-start.14
  476.8 5.9 all-to-all-done.14
  482.7 7.3 %all-to-all-start.10 = ((bf16[4,1024,256]{2,1,0:T(8,128)(2,1)}), bf16[4,1024,256]{2,1,0:T(8,128)(2,1)}, u32[]{:S(2)}, u32[]{:S(2)}) async-start(bf16[4,1024,256]{2,1,0:T(8,128)(2,1)} %bitcast.490), calls=%async_computation.10 | async-start | bytes 4194304 | tf_op jit(solution)/shard_map/all_to_all | solution.py:540
  495.9 24.5 %collective-permute-done.20 = bf16[128,1024]{1,0:T(8,128)(2,1)S(1)} collective-permute-done((bf16[128,1024]{1,0:T(8,128)(2,1)S(1)}, bf16[128,1024]{1,0:T(8,128)(2,1)S(1)}, u32[]{:S(2)}, u32[]{:S(2)}) %collective-permute-start.20) | collective-permute-done | bytes 262176 | tf_op jit(solution)/shard_map/ppermute | solution.py:357
  523.3 5.3 collective-permute-done.21
  532.4 3.0 slice_bitcast_fusion.32
  542.0 9.5 %self_backward.1 = (bf16[4,2,64,512]{3,2,1,0:T(8,128)(2,1)S(1)}, f32[8,256]{1,0:T(8,128)S(1)}) custom-call(bf16[4,2,64,512]{3,2,1,0:T(8,128)(2,1)S(1)} %bitcast.498, bf16[4,2,64,256]{3,2,1,0:T(8,128)(2,1)S(1)} %bitcast.502, s32[2,256,1]{2,1,0:T(8,128)S(1)} %broadcast_in_dim_squeeze.4.seg_col_ref.seg_ref, s32[2,1,256]{2,1,0:T(1,128)S(1)} %copy-done.6, ...), custom_call_target="tpu_custom_call" | custom-call | flops 335544320 | bytes 3145728 | tf_op jit(solution)/shard_map/self_backward/pallas_call | solution.py:264
  557.4 4.6 all-to-all-start.13
  562.0 6.7 convolution_bitcast_fusion
  570.4 4.5 all-to-all-done.13
  580.9 2.7 collective-permute-start.24
  584.1 7.8 %collective-permute-done.30 = bf16[40,1024]{1,0:T(8,128)(2,1)S(1)} collective-permute-done((bf16[40,1024]{1,0:T(8,128)(2,1)S(1)}, bf16[40,1024]{1,0:T(8,128)(2,1)S(1)}, u32[]{:S(2)}, u32[]{:S(2)}) %collective-permute-start.30) | collective-permute-done | bytes 81952 | tf_op jit(solution)/shard_map/ppermute | solution.py:357
  598.7 5.8 all-to-all-start.11
  604.6 8.8 %all-to-all-done.11 = f32[32,8,128]{2,1,0:T(8,128)S(1)} async-done(((f32[32,8,128]{2,1,0:T(8,128)}), f32[32,8,128]{2,1,0:T(8,128)S(1)}, u32[]{:S(2)}, u32[]{:S(2)}) %all-to-all-start.11) | async-done | bytes 131104 | tf_op jit(solution)/shard_map/all_to_all | solution.py:574
  613.4 5.0 all-to-all-start.12
  621.7 3.2 collective-permute-done.25
  629.9 5.5 all-to-all-done.12
  636.9 3.3 fusion.14
  640.2 8.1 %all-to-all-start.17 = ((bf16[32,32,512]{2,1,0:T(8,128)(2,1)}), bf16[32,32,512]{2,1,0:T(8,128)(2,1)S(1)}, u32[]{:S(2)}, u32[]{:S(2)}) async-start(bf16[32,32,512]{2,1,0:T(8,128)(2,1)} %bitcast.190), calls=%async_computation.17 | async-start | bytes 2097152 | tf_op jit(solution)/shard_map/all_to_all | solution.py:394
  650.6 15.7 %all-to-all-done.17 = bf16[32,32,512]{2,1,0:T(8,128)(2,1)S(1)} async-done(((bf16[32,32,512]{2,1,0:T(8,128)(2,1)}), bf16[32,32,512]{2,1,0:T(8,128)(2,1)S(1)}, u32[]{:S(2)}, u32[]{:S(2)}) %all-to-all-start.17) | async-done | bytes 1048608 | tf_op jit(solution)/shard_map/all_to_all | solution.py:394
  669.4 3.1 collective-permute-start.36
  (421 shorter events, 222.9 us)
Async XLA Ops:
  0.7 111.4 %copy-start = (bf16[2,1,4,128,1024]{4,3,2,1,0:T(8,128)(2,1)S(1)}, bf16[2,1,4,128,1024]{4,3,2,1,0:T(8,128)(2,1)}, u32[]{:S(2)}) copy-start(bf16[2,1,4,128,1024]{4,3,2,1,0:T(8,128)(2,1)} %param.23) | copy-start | bytes 6291460
  0.7 37.1 %copy-start.6 = (s32[2,1,256]{2,1,0:T(1,128)S(1)}, s32[2,1,256]{2,1,0:T(1,128)}, u32[]{:S(2)}) copy-start(s32[2,1,256]{2,1,0:T(1,128)} %seg_row_ref.3) | copy-start | bytes 6148
  0.7 37.4 %copy-start.57 = (bf16[32,512]{1,0:T(8,128)(2,1)S(1)}, bf16[32,512]{1,0:T(8,128)(2,1)}, u32[]{:S(2)}) copy-start(bf16[32,512]{1,0:T(8,128)(2,1)} %param.36) | copy-start | bytes 98308
  2.4 19.1 %collective-permute-start.2 = (bf16[40,1024]{1,0:T(8,128)(2,1)S(1)}, bf16[40,1024]{1,0:T(8,128)(2,1)S(1)}, u32[]{:S(2)}, u32[]{:S(2)}) collective-permute-start(bf16[40,1024]{1,0:T(8,128)(2,1)S(1)} %pad_maximum_fusion.3), channel_id=1, source_target_pairs={{0,0},{1,4},{2,8},{3,12},{4,16},{5,20},{6,24},{7,28},{8,32},{9,36}... | collective-permute-start | bytes 245768 | tf_op jit(solution)/shard_map/ppermute | solution.py:451
  12.8 17.4 %all-to-all-start = ((bf16[32,8,128]{2,1,0:T(8,128)(2,1)}), bf16[32,8,128]{2,1,0:T(8,128)(2,1)S(1)}, u32[]{:S(2)}, u32[]{:S(2)}) async-start(bf16[32,8,128]{2,1,0:T(8,128)(2,1)} %broadcast_in_dim_broadcast_in_dim_broadcast_in_dim.2), calls=%async_computation | async-start | bytes 131072 | tf_op jit(solution)/shard_map/all_to_all | solution.py:388
  31.0 16.8 %all-to-all-start.2 = ((bf16[32,8,1024]{2,1,0:T(8,128)(2,1)}), bf16[32,8,1024]{2,1,0:T(8,128)(2,1)S(1)}, u32[]{:S(2)}, u32[]{:S(2)}) async-start(bf16[32,8,1024]{2,1,0:T(8,128)(2,1)} %broadcast_in_dim.21), calls=%async_computation.2 | async-start | bytes 1048576 | tf_op jit(solution)/shard_map/all_to_all | solution.py:388
  35.0 22.8 %collective-permute-start = (bf16[128,1024]{1,0:T(8,128)(2,1)S(1)}, bf16[128,1024]{1,0:T(8,128)(2,1)S(1)}, u32[]{:S(2)}, u32[]{:S(2)}) collective-permute-start(bf16[128,1024]{1,0:T(8,128)(2,1)S(1)} %bitcast.503), channel_id=1, source_target_pairs={{0,64},{32,96},{64,0},{96,32},{1,65},{33,97},{65,1},{97,33},{2,66}... | collective-permute-start | bytes 786440 | tf_op jit(solution)/shard_map/ppermute | solution.py:357
  49.7 21.8 %all-to-all-start.1 = ((bf16[32,32,512]{2,1,0:T(8,128)(2,1)}), bf16[32,32,512]{2,1,0:T(8,128)(2,1)}, u32[]{:S(2)}, u32[]{:S(2)}) async-start(bf16[32,32,512]{2,1,0:T(8,128)(2,1)} %broadcast_in_dim.20), calls=%async_computation.1 | async-start | bytes 2097152 | tf_op jit(solution)/shard_map/all_to_all | solution.py:388
  58.6 3.6 collective-permute-start.1
  73.0 31.7 %all-to-all-start.4 = ((bf16[32,32,1024]{2,1,0:T(8,128)(2,1)}), bf16[32,32,1024]{2,1,0:T(8,128)(2,1)}, u32[]{:S(2)}, u32[]{:S(2)}) async-start(bf16[32,32,1024]{2,1,0:T(8,128)(2,1)} %broadcast_in_dim.24), calls=%async_computation.4 | async-start | bytes 4194304 | tf_op jit(solution)/shard_map/all_to_all | solution.py:388
  88.4 4.5 collective-permute-start.3
  96.1 52.8 %collective-permute-start.4 = (bf16[128,1024]{1,0:T(8,128)(2,1)}, bf16[128,1024]{1,0:T(8,128)(2,1)}, u32[]{:S(2)}, u32[]{:S(2)}) collective-permute-start(bf16[128,1024]{1,0:T(8,128)(2,1)} %fusion.70), channel_id=1, source_target_pairs={{0,64},{32,96},{64,0},{96,32},{1,65},{33,97},{65,1},{97,33},{2,66}... | collective-permute-start | bytes 786440 | tf_op jit(solution)/shard_map/ppermute | solution.py:357
  105.6 17.8 %all-to-all-start.3 = ((bf16[32,32,256]{2,1,0:T(8,128)(2,1)}), bf16[32,32,256]{2,1,0:T(8,128)(2,1)S(1)}, u32[]{:S(2)}, u32[]{:S(2)}) async-start(bf16[32,32,256]{2,1,0:T(8,128)(2,1)} %broadcast_in_dim.22), calls=%async_computation.3 | async-start | bytes 1048576 | tf_op jit(solution)/shard_map/all_to_all | solution.py:388
  124.4 15.9 %all-to-all-start.6 = ((bf16[32,8,1024]{2,1,0:T(8,128)(2,1)}), bf16[32,8,1024]{2,1,0:T(8,128)(2,1)}, u32[]{:S(2)}, u32[]{:S(2)}) async-start(bf16[32,8,1024]{2,1,0:T(8,128)(2,1)} %broadcast_in_dim.25), calls=%async_computation.6 | async-start | bytes 1048576 | tf_op jit(solution)/shard_map/all_to_all | solution.py:388
  140.3 44.9 %all-to-all-start.5 = ((bf16[4,1024,256]{1,2,0:T(8,128)(2,1)}), bf16[4,1024,256]{1,2,0:T(8,128)(2,1)}, u32[]{:S(2)}, u32[]{:S(2)}) async-start(bf16[4,1024,256]{1,2,0:T(8,128)(2,1)} %pad_maximum_fusion), calls=%async_computation.5 | async-start | bytes 4194304 | tf_op jit(solution)/shard_map/all_to_all | solution.py:491
  151.1 28.4 %collective-permute-start.5 = (bf16[128,1024]{1,0:T(8,128)(2,1)}, bf16[128,1024]{1,0:T(8,128)(2,1)}, u32[]{:S(2)}, u32[]{:S(2)}) collective-permute-start(bf16[128,1024]{1,0:T(8,128)(2,1)} %multiply_convert_fusion.4), channel_id=1, source_target_pairs={{0,64},{32,96},{64,0},{96,32},{1,65},{33,97},{65,1},{97,33},{2,66}... | collective-permute-start | bytes 786440 | tf_op jit(solution)/shard_map/ppermute | solution.py:357
  181.4 11.4 %collective-permute-start.6 = (bf16[2,128,1024]{2,1,0:T(8,128)(2,1)}, bf16[2,128,1024]{2,1,0:T(8,128)(2,1)}, u32[]{:S(2)}, u32[]{:S(2)}) collective-permute-start(bf16[2,128,1024]{2,1,0:T(8,128)(2,1)} %maximum_select_fusion.8), channel_id=1, source_target_pairs={{0,32},{32,0},{64,96},{96,64},{1,33},{33,1},{65,97},{97,65},{2,34}... | collective-permute-start | bytes 1572872 | tf_op jit(solution)/shard_map/ppermute | solution.py:361
  186.7 32.8 %all-to-all-start.7 = ((bf16[32,32,704]{2,1,0:T(8,128)(2,1)}), bf16[32,32,704]{2,1,0:T(8,128)(2,1)}, u32[]{:S(2)}, u32[]{:S(2)}) async-start(bf16[32,32,704]{2,1,0:T(8,128)(2,1)} %broadcast_in_dim.26), calls=%async_computation.7 | async-start | bytes 3145728 | tf_op jit(solution)/shard_map/all_to_all | solution.py:388
  219.5 11.1 %collective-permute-start.7 = (bf16[2,128,1024]{2,1,0:T(8,128)(2,1)}, bf16[2,128,1024]{2,1,0:T(8,128)(2,1)}, u32[]{:S(2)}, u32[]{:S(2)}) collective-permute-start(bf16[2,128,1024]{2,1,0:T(8,128)(2,1)} %fusion.49), channel_id=1, source_target_pairs={{0,32},{32,0},{64,96},{96,64},{1,33},{33,1},{65,97},{97,65},{2,34}... | collective-permute-start | bytes 1572872 | tf_op jit(solution)/shard_map/ppermute | solution.py:361
  220.8 43.7 %all-to-all-start.9 = ((bf16[32,24,1024]{2,1,0:T(8,128)(2,1)}), bf16[32,24,1024]{2,1,0:T(8,128)(2,1)}, u32[]{:S(2)}, u32[]{:S(2)}) async-start(bf16[32,24,1024]{2,1,0:T(8,128)(2,1)} %broadcast_in_dim.28), calls=%async_computation.9 | async-start | bytes 3145728 | tf_op jit(solution)/shard_map/all_to_all | solution.py:388
  230.4 24.0 %collective-permute-start.13 = (bf16[128,1024]{1,0:T(8,128)(2,1)}, bf16[128,1024]{1,0:T(8,128)(2,1)}, u32[]{:S(2)}, u32[]{:S(2)}) collective-permute-start(bf16[128,1024]{1,0:T(8,128)(2,1)} %bitcast.522), channel_id=1, source_target_pairs={{0,64},{32,96},{64,0},{96,32},{1,65},{33,97},{65,1},{97,33},{2,66}... | collective-permute-start | bytes 786440 | tf_op jit(solution)/shard_map/ppermute | solution.py:357
  233.8 26.2 %collective-permute-start.8 = (bf16[128,1024]{1,0:T(8,128)(2,1)}, bf16[128,1024]{1,0:T(8,128)(2,1)}, u32[]{:S(2)}, u32[]{:S(2)}) collective-permute-start(bf16[128,1024]{1,0:T(8,128)(2,1)} %fusion.71), channel_id=1, source_target_pairs={{0,64},{32,96},{64,0},{96,32},{1,65},{33,97},{65,1},{97,33},{2,66}... | collective-permute-start | bytes 786440 | tf_op jit(solution)/shard_map/ppermute | solution.py:357
  256.5 24.5 %collective-permute-start.14 = (bf16[2,128,1024]{2,1,0:T(8,128)(2,1)}, bf16[2,128,1024]{2,1,0:T(8,128)(2,1)}, u32[]{:S(2)}, u32[]{:S(2)}) collective-permute-start(bf16[2,128,1024]{2,1,0:T(8,128)(2,1)} %maximum_select_fusion.11), channel_id=1, source_target_pairs={{0,32},{32,0},{64,96},{96,64},{1,33},{33,1},{65,97},{97,65},{2,34}... | collective-permute-start | bytes 1572872 | tf_op jit(solution)/shard_map/ppermute | solution.py:361
  263.1 14.0 %collective-permute-start.9 = (bf16[128,1024]{1,0:T(8,128)(2,1)}, bf16[128,1024]{1,0:T(8,128)(2,1)}, u32[]{:S(2)}, u32[]{:S(2)}) collective-permute-start(bf16[128,1024]{1,0:T(8,128)(2,1)} %multiply_convert_fusion.3), channel_id=1, source_target_pairs={{0,64},{32,96},{64,0},{96,32},{1,65},{33,97},{65,1},{97,33},{2,66}... | collective-permute-start | bytes 786440 | tf_op jit(solution)/shard_map/ppermute | solution.py:357
  265.9 32.8 %all-to-all-start.8 = ((bf16[32,32,704]{2,1,0:T(8,128)(2,1)}), bf16[32,32,704]{2,1,0:T(8,128)(2,1)}, u32[]{:S(2)}, u32[]{:S(2)}) async-start(bf16[32,32,704]{2,1,0:T(8,128)(2,1)} %broadcast_in_dim.27), calls=%async_computation.8 | async-start | bytes 3145728 | tf_op jit(solution)/shard_map/all_to_all | solution.py:388
  278.1 9.1 %collective-permute-start.10 = (bf16[2,128,1024]{2,1,0:T(8,128)(2,1)S(1)}, bf16[2,128,1024]{2,1,0:T(8,128)(2,1)S(1)}, u32[]{:S(2)}, u32[]{:S(2)}) collective-permute-start(bf16[2,128,1024]{2,1,0:T(8,128)(2,1)S(1)} %maximum_select_fusion.9), channel_id=1, source_target_pairs={{0,32},{32,0},{64,96},{96,64},{1,33},{33,1},{65,97},{97,65},{2,34}... | collective-permute-start | bytes 1572872 | tf_op jit(solution)/shard_map/ppermute | solution.py:361
  309.3 28.0 %all-to-all-start.18 = ((bf16[32,32,704]{2,1,0:T(8,128)(2,1)}), bf16[32,32,704]{2,1,0:T(8,128)(2,1)}, u32[]{:S(2)}, u32[]{:S(2)}) async-start(bf16[32,32,704]{2,1,0:T(8,128)(2,1)} %convolution_convert_fusion.1), calls=%async_computation.18 | async-start | bytes 3145728 | tf_op jit(solution)/shard_map/all_to_all | solution.py:394
  325.9 24.3 %collective-permute-start.15 = (bf16[2,128,1024]{2,1,0:T(8,128)(2,1)}, bf16[2,128,1024]{2,1,0:T(8,128)(2,1)}, u32[]{:S(2)}, u32[]{:S(2)}) collective-permute-start(bf16[2,128,1024]{2,1,0:T(8,128)(2,1)} %fusion.50), channel_id=1, source_target_pairs={{0,32},{32,0},{64,96},{96,64},{1,33},{33,1},{65,97},{97,65},{2,34}... | collective-permute-start | bytes 1572872 | tf_op jit(solution)/shard_map/ppermute | solution.py:361
  337.3 29.1 %all-to-all-start.19 = ((bf16[32,32,704]{2,1,0:T(8,128)(2,1)}), bf16[32,32,704]{2,1,0:T(8,128)(2,1)}, u32[]{:S(2)}, u32[]{:S(2)}) async-start(bf16[32,32,704]{2,1,0:T(8,128)(2,1)} %convolution_convert_fusion), calls=%async_computation.19 | async-start | bytes 3145728 | tf_op jit(solution)/shard_map/all_to_all | solution.py:394
  346.5 6.7 collective-permute-start.11
  353.1 18.5 %collective-permute-start.16 = (bf16[128,1024]{1,0:T(8,128)(2,1)}, bf16[128,1024]{1,0:T(8,128)(2,1)}, u32[]{:S(2)}, u32[]{:S(2)}) collective-permute-start(bf16[128,1024]{1,0:T(8,128)(2,1)} %fusion.73), channel_id=1, source_target_pairs={{0,64},{32,96},{64,0},{96,32},{1,65},{33,97},{65,1},{97,33},{2,66}... | collective-permute-start | bytes 786440 | tf_op jit(solution)/shard_map/ppermute | solution.py:357
  354.6 20.1 %collective-permute-start.12 = (bf16[128,1024]{1,0:T(8,128)(2,1)}, bf16[128,1024]{1,0:T(8,128)(2,1)}, u32[]{:S(2)}, u32[]{:S(2)}) collective-permute-start(bf16[128,1024]{1,0:T(8,128)(2,1)} %fusion.72), channel_id=1, source_target_pairs={{0,64},{32,96},{64,0},{96,32},{1,65},{33,97},{65,1},{97,33},{2,66}... | collective-permute-start | bytes 786440 | tf_op jit(solution)/shard_map/ppermute | solution.py:357
  366.5 45.3 %all-to-all-start.15 = ((bf16[32,24,1024]{2,1,0:T(8,128)(2,1)}), bf16[32,24,1024]{2,1,0:T(8,128)(2,1)}, u32[]{:S(2)}, u32[]{:S(2)}) async-start(bf16[32,24,1024]{2,1,0:T(8,128)(2,1)} %bitcast.508), calls=%async_computation.15 | async-start | bytes 3145728 | tf_op jit(solution)/shard_map/all_to_all | solution.py:394
  377.5 19.3 %collective-permute-start.17 = (bf16[128,1024]{1,0:T(8,128)(2,1)}, bf16[128,1024]{1,0:T(8,128)(2,1)}, u32[]{:S(2)}, u32[]{:S(2)}) collective-permute-start(bf16[128,1024]{1,0:T(8,128)(2,1)} %get-tuple-element.126), channel_id=1, source_target_pairs={{0,64},{32,96},{64,0},{96,32},{1,65},{33,97},{65,1},{97,33},{2,66}... | collective-permute-start | bytes 786440 | tf_op jit(solution)/shard_map/ppermute | solution.py:357
  398.8 16.1 %collective-permute-start.18 = (bf16[2,128,1024]{2,1,0:T(8,128)(2,1)}, bf16[2,128,1024]{2,1,0:T(8,128)(2,1)}, u32[]{:S(2)}, u32[]{:S(2)}) collective-permute-start(bf16[2,128,1024]{2,1,0:T(8,128)(2,1)} %maximum_select_fusion.13), channel_id=1, source_target_pairs={{0,32},{32,0},{64,96},{96,64},{1,33},{33,1},{65,97},{97,65},{2,34}... | collective-permute-start | bytes 1572872 | tf_op jit(solution)/shard_map/ppermute | solution.py:361
  401.4 5.4 collective-permute-start.37
  406.6 3.0 collective-permute-start.39
  406.8 7.3 %collective-permute-start.38 = (bf16[2,32,704]{2,1,0:T(8,128)(2,1)S(1)}, bf16[2,32,704]{2,1,0:T(8,128)(2,1)S(1)}, u32[]{:S(2)}, u32[]{:S(2)}) collective-permute-start(bf16[2,32,704]{2,1,0:T(8,128)(2,1)S(1)} %maximum_select_fusion.22), channel_id=1, source_target_pairs={{0,32},{32,0},{64,96},{96,64},{1,33},{33,1},{65,97},{97,65},{2,34}... | collective-permute-start | bytes 270344 | tf_op jit(solution)/shard_map/ppermute | solution.py:361
  410.3 60.7 %collective-permute-start.40 = (bf16[2,32,704]{2,1,0:T(8,128)(2,1)}, bf16[2,32,704]{2,1,0:T(8,128)(2,1)}, u32[]{:S(2)}, u32[]{:S(2)}) collective-permute-start(bf16[2,32,704]{2,1,0:T(8,128)(2,1)} %maximum_select_fusion.23), channel_id=1, source_target_pairs={{0,32},{32,0},{64,96},{96,64},{1,33},{33,1},{65,97},{97,65},{2,34}... | collective-permute-start | bytes 270344 | tf_op jit(solution)/shard_map/ppermute | solution.py:361
  444.8 21.6 %all-to-all-start.16 = ((bf16[32,32,256]{2,1,0:T(8,128)(2,1)}), bf16[32,32,256]{2,1,0:T(8,128)(2,1)S(1)}, u32[]{:S(2)}, u32[]{:S(2)}) async-start(bf16[32,32,256]{2,1,0:T(8,128)(2,1)} %convolution_convert_fusion.4), calls=%async_computation.16 | async-start | bytes 1048576 | tf_op jit(solution)/shard_map/all_to_all | solution.py:394
  457.3 33.8 %collective-permute-start.19 = (bf16[2,128,1024]{2,1,0:T(8,128)(2,1)}, bf16[2,128,1024]{2,1,0:T(8,128)(2,1)}, u32[]{:S(2)}, u32[]{:S(2)}) collective-permute-start(bf16[2,128,1024]{2,1,0:T(8,128)(2,1)} %fusion.51), channel_id=1, source_target_pairs={{0,32},{32,0},{64,96},{96,64},{1,33},{33,1},{65,97},{97,65},{2,34}... | collective-permute-start | bytes 1572872 | tf_op jit(solution)/shard_map/ppermute | solution.py:361
  466.4 16.3 %all-to-all-start.14 = ((bf16[32,8,1024]{2,1,0:T(8,128)(2,1)}), bf16[32,8,1024]{2,1,0:T(8,128)(2,1)}, u32[]{:S(2)}, u32[]{:S(2)}) async-start(bf16[32,8,1024]{2,1,0:T(8,128)(2,1)} %convolution_convert_fusion.5), calls=%async_computation.14 | async-start | bytes 1048576 | tf_op jit(solution)/shard_map/all_to_all | solution.py:394
  476.5 17.7 %collective-permute-start.32 = (bf16[32,256]{1,0:T(8,128)(2,1)S(1)}, bf16[32,256]{1,0:T(8,128)(2,1)S(1)}, u32[]{:S(2)}, u32[]{:S(2)}) collective-permute-start(bf16[32,256]{1,0:T(8,128)(2,1)S(1)} %reduce_sum.211), channel_id=1, source_target_pairs={{0,64},{32,96},{64,0},{96,32},{1,65},{33,97},{65,1},{97,33},{2,66}... | collective-permute-start | bytes 49160 | tf_op jit(solution)/shard_map/ppermute | solution.py:357
  482.7 49.8 %all-to-all-start.10 = ((bf16[4,1024,256]{2,1,0:T(8,128)(2,1)}), bf16[4,1024,256]{2,1,0:T(8,128)(2,1)}, u32[]{:S(2)}, u32[]{:S(2)}) async-start(bf16[4,1024,256]{2,1,0:T(8,128)(2,1)} %bitcast.490), calls=%async_computation.10 | async-start | bytes 4194304 | tf_op jit(solution)/shard_map/all_to_all | solution.py:540
  492.8 27.6 %collective-permute-start.20 = (bf16[128,1024]{1,0:T(8,128)(2,1)S(1)}, bf16[128,1024]{1,0:T(8,128)(2,1)S(1)}, u32[]{:S(2)}, u32[]{:S(2)}) collective-permute-start(bf16[128,1024]{1,0:T(8,128)(2,1)S(1)} %fusion.74), channel_id=1, source_target_pairs={{0,64},{32,96},{64,0},{96,32},{1,65},{33,97},{65,1},{97,33},{2,66}... | collective-permute-start | bytes 786440 | tf_op jit(solution)/shard_map/ppermute | solution.py:357
  494.2 1.6 collective-permute-start.33
  521.6 6.9 %collective-permute-start.21 = (bf16[128,1024]{1,0:T(8,128)(2,1)S(1)}, bf16[128,1024]{1,0:T(8,128)(2,1)S(1)}, u32[]{:S(2)}, u32[]{:S(2)}) collective-permute-start(bf16[128,1024]{1,0:T(8,128)(2,1)S(1)} %get-tuple-element.124), channel_id=1, source_target_pairs={{0,64},{32,96},{64,0},{96,32},{1,65},{33,97},{65,1},{97,33},{2,66}... | collective-permute-start | bytes 786440 | tf_op jit(solution)/shard_map/ppermute | solution.py:357
  529.4 9.9 %collective-permute-start.22 = (bf16[2,128,1024]{2,1,0:T(8,128)(2,1)}, bf16[2,128,1024]{2,1,0:T(8,128)(2,1)}, u32[]{:S(2)}, u32[]{:S(2)}) collective-permute-start(bf16[2,128,1024]{2,1,0:T(8,128)(2,1)} %maximum_select_fusion.14), channel_id=1, source_target_pairs={{0,32},{32,0},{64,96},{96,64},{1,33},{33,1},{65,97},{97,65},{2,34}... | collective-permute-start | bytes 1572872 | tf_op jit(solution)/shard_map/ppermute | solution.py:361
  539.1 97.8 %collective-permute-start.34 = (bf16[1024,512]{1,0:T(8,128)(2,1)}, bf16[1024,512]{1,0:T(8,128)(2,1)}, u32[]{:S(2)}, u32[]{:S(2)}) collective-permute-start(bf16[1024,512]{1,0:T(8,128)(2,1)} %fusion.37), channel_id=1, source_target_pairs={{0,32},{32,0},{64,96},{96,64},{1,33},{33,1},{65,97},{97,65},{2,34}... | collective-permute-start | bytes 3145736 | tf_op jit(solution)/shard_map/ppermute | solution.py:361
  555.8 22.7 %collective-permute-start.23 = (bf16[2,128,1024]{2,1,0:T(8,128)(2,1)}, bf16[2,128,1024]{2,1,0:T(8,128)(2,1)}, u32[]{:S(2)}, u32[]{:S(2)}) collective-permute-start(bf16[2,128,1024]{2,1,0:T(8,128)(2,1)} %fusion.53), channel_id=1, source_target_pairs={{0,32},{32,0},{64,96},{96,64},{1,33},{33,1},{65,97},{97,65},{2,34}... | collective-permute-start | bytes 1572872 | tf_op jit(solution)/shard_map/ppermute | solution.py:361
  557.4 17.5 %all-to-all-start.13 = ((bf16[32,8,1024]{2,1,0:T(8,128)(2,1)}), bf16[32,8,1024]{2,1,0:T(8,128)(2,1)}, u32[]{:S(2)}, u32[]{:S(2)}) async-start(bf16[32,8,1024]{2,1,0:T(8,128)(2,1)} %convolution_convert_fusion.6), calls=%async_computation.13 | async-start | bytes 1048576 | tf_op jit(solution)/shard_map/all_to_all | solution.py:394
  576.1 7.5 %collective-permute-start.29 = (bf16[40,1024]{1,0:T(8,128)(2,1)S(1)}, bf16[40,1024]{1,0:T(8,128)(2,1)S(1)}, u32[]{:S(2)}, u32[]{:S(2)}) collective-permute-start(bf16[40,1024]{1,0:T(8,128)(2,1)S(1)} %pad_maximum_fusion.4), channel_id=1, source_target_pairs={{0,0},{4,1},{8,2},{12,3},{16,4},{20,5},{24,6},{28,7},{32,8},{36,9}... | collective-permute-start | bytes 245768 | tf_op jit(solution)/shard_map/ppermute | solution.py:586
  580.9 14.9 %collective-permute-start.24 = (bf16[128,1024]{1,0:T(8,128)(2,1)}, bf16[128,1024]{1,0:T(8,128)(2,1)}, u32[]{:S(2)}, u32[]{:S(2)}) collective-permute-start(bf16[128,1024]{1,0:T(8,128)(2,1)} %fusion.75), channel_id=1, source_target_pairs={{0,64},{32,96},{64,0},{96,32},{1,65},{33,97},{65,1},{97,33},{2,66}... | collective-permute-start | bytes 786440 | tf_op jit(solution)/shard_map/ppermute | solution.py:357
  583.6 8.4 %collective-permute-start.30 = (bf16[40,1024]{1,0:T(8,128)(2,1)S(1)}, bf16[40,1024]{1,0:T(8,128)(2,1)S(1)}, u32[]{:S(2)}, u32[]{:S(2)}) collective-permute-start(bf16[40,1024]{1,0:T(8,128)(2,1)S(1)} %collective-permute-done.29), channel_id=1, source_target_pairs={{0,64},{32,96},{64,0},{96,32},{1,65},{33,97},{65,1},{97,33},{2,66}... | collective-permute-start | bytes 245768 | tf_op jit(solution)/shard_map/ppermute | solution.py:357
  593.3 27.2 %collective-permute-start.31 = (bf16[2,40,1024]{2,1,0:T(8,128)(2,1)}, bf16[2,40,1024]{2,1,0:T(8,128)(2,1)}, u32[]{:S(2)}, u32[]{:S(2)}) collective-permute-start(bf16[2,40,1024]{2,1,0:T(8,128)(2,1)} %maximum_select_fusion.19), channel_id=1, source_target_pairs={{0,32},{32,0},{64,96},{96,64},{1,33},{33,1},{65,97},{97,65},{2,34}... | collective-permute-start | bytes 491528 | tf_op jit(solution)/shard_map/ppermute | solution.py:361
  598.7 14.7 %all-to-all-start.11 = ((f32[32,8,128]{2,1,0:T(8,128)}), f32[32,8,128]{2,1,0:T(8,128)S(1)}, u32[]{:S(2)}, u32[]{:S(2)}) async-start(f32[32,8,128]{2,1,0:T(8,128)} %broadcast_in_dim.29), calls=%async_computation.11 | async-start | bytes 262144 | tf_op jit(solution)/shard_map/all_to_all | solution.py:574
  613.4 22.1 %all-to-all-start.12 = ((bf16[32,32,512]{2,1,0:T(8,128)(2,1)}), bf16[32,32,512]{2,1,0:T(8,128)(2,1)}, u32[]{:S(2)}, u32[]{:S(2)}) async-start(bf16[32,32,512]{2,1,0:T(8,128)(2,1)} %convolution_convert_fusion.3), calls=%async_computation.12 | async-start | bytes 2097152 | tf_op jit(solution)/shard_map/all_to_all | solution.py:394
  621.6 3.3 collective-permute-start.25
  624.9 3.8 collective-permute-start.26
  636.8 11.5 %collective-permute-start.27 = (bf16[32,512]{1,0:T(8,128)(2,1)S(1)}, bf16[32,512]{1,0:T(8,128)(2,1)S(1)}, u32[]{:S(2)}, u32[]{:S(2)}) collective-permute-start(bf16[32,512]{1,0:T(8,128)(2,1)S(1)} %reduce_sum.207), channel_id=1, source_target_pairs={{0,64},{32,96},{64,0},{96,32},{1,65},{33,97},{65,1},{97,33},{2,66}... | collective-permute-start | bytes 98312 | tf_op jit(solution)/shard_map/ppermute | solution.py:357
  640.2 26.2 %all-to-all-start.17 = ((bf16[32,32,512]{2,1,0:T(8,128)(2,1)}), bf16[32,32,512]{2,1,0:T(8,128)(2,1)S(1)}, u32[]{:S(2)}, u32[]{:S(2)}) async-start(bf16[32,32,512]{2,1,0:T(8,128)(2,1)} %bitcast.190), calls=%async_computation.17 | async-start | bytes 2097152 | tf_op jit(solution)/shard_map/all_to_all | solution.py:394
  648.4 1.5 collective-permute-start.28
  666.5 2.8 collective-permute-start.35
  669.4 4.0 collective-permute-start.36
  (65 other events, 550.0 us)

commit v2 on v1

--- a/solution.py
+++ b/solution.py
@@ -395,6 +395,196 @@
     return jnp.sum(sent.astype(f32), axis=0)
 
 
+MESH = pl.DeviceIdType.MESH
+
+
+def remote(source, target, send_sem, recv_sem, device):
+    return pltpu.make_async_remote_copy(
+        src_ref=source,
+        dst_ref=target,
+        send_sem=send_sem,
+        recv_sem=recv_sem,
+        device_id=device,
+        device_id_type=MESH,
+    )
+
+
+def meet(devices):
+    barrier = pltpu.get_barrier_semaphore()
+    for device in devices:
+        pl.semaphore_signal(barrier, inc=1, device_id=device, device_id_type=MESH)
+    pl.semaphore_wait(barrier, len(devices))
+
+
+class Ring:
+    def __init__(self, group, half, me, device_at, send_sems, recv_sems):
+        right, left = lax.rem(me + 1, 4), lax.rem(me + 3, 4)
+        to_right, to_left = device_at(right), device_at(left)
+
+        def copy(ref, device, i):
+            return remote(ref, ref, send_sems.at[i], recv_sems.at[i], device)
+
+        self.direct = [copy(group(me), to_right, 0), copy(group(me), to_left, 1)]
+        self.passed = [copy(half(left, 0), to_right, 2), copy(half(right, 1), to_left, 3)]
+
+    def start(self):
+        for copy in self.direct:
+            copy.start()
+
+    def forward(self):
+        for arrived, onward in zip(self.direct, self.passed):
+            arrived.wait_recv()
+            onward.start()
+
+    def finish(self):
+        for copy in self.passed:
+            copy.wait_recv()
+
+    def drain(self):
+        for copy in self.direct + self.passed:
+            copy.wait_send()
+
+
+def gather_kernel(first_x, split, n_rep, *refs):
+    n = len(first_x)
+    blocks, own_rows = refs[:n], refs[n : n + n_rep]
+    wholes, all_rows = refs[n + n_rep : 2 * n + n_rep], refs[2 * n + n_rep : 2 * n + 2 * n_rep]
+    local_sems, pair_send, pair_recv, ring_send, ring_recv, rep_send, rep_recv = refs[2 * n + 2 * n_rep :]
+    at = lax.axis_index("shard")
+    rep = lax.axis_index("rep")
+    x, y, z = lax.div(at, 8), lax.rem(lax.div(at, 2), 4), lax.rem(at, 2)
+    chip, core = lax.div(rep, 2), lax.rem(rep, 2)
+    pair = {"shard": at + 1 - 2 * z}
+    far = {"rep": (1 - chip) * 2 + core}
+    near = {"rep": chip * 2 + 1 - core}
+
+    def on_x(i):
+        return {"shard": i * 8 + y * 2 + z}
+
+    def on_y(i):
+        return {"shard": x * 8 + i * 2 + z}
+
+    meet(
+        [pair, far, near]
+        + [on_x(lax.rem(x + d, 4)) for d in (1, 3)]
+        + [on_y(lax.rem(y + d, 4)) for d in (1, 3)]
+    )
+    locals_, pairs, small_rings, large_rings = [], [], [], []
+    for i in range(n):
+        whole = wholes[i].at[core] if split[i] else wholes[i]
+        slot = whole.at[x, y, z]
+        locals_.append(pltpu.make_async_copy(blocks[i], slot, local_sems.at[i]))
+        pairs.append(remote(blocks[i], slot, pair_send.at[i], pair_recv.at[i], pair))
+
+        def x_small(j, whole=whole):
+            return whole.at[j, y]
+
+        def x_small_half(j, h, whole=whole):
+            return whole.at[j, y, h]
+
+        def y_small(j, whole=whole):
+            return whole.at[x, j]
+
+        def y_small_half(j, h, whole=whole):
+            return whole.at[x, j, h]
+
+        def x_large(j, whole=whole):
+            return whole.at[j]
+
+        def x_large_half(j, h, whole=whole):
+            return whole.at[j, pl.ds(2 * h, 2)]
+
+        def y_large(j, whole=whole):
+            return whole.at[:, j]
+
+        def y_large_half(j, h, whole=whole):
+            return whole.at[pl.ds(2 * h, 2), j]
+
+        small, large = ring_send.at[i, 0], ring_send.at[i, 1]
+        small_in, large_in = ring_recv.at[i, 0], ring_recv.at[i, 1]
+        if first_x[i]:
+            small_rings.append(Ring(x_small, x_small_half, x, on_x, small, small_in))
+            large_rings.append(Ring(y_large, y_large_half, y, on_y, large, large_in))
+        else:
+            small_rings.append(Ring(y_small, y_small_half, y, on_y, small, small_in))
+            large_rings.append(Ring(x_large, x_large_half, x, on_x, large, large_in))
+    for i in range(n):
+        locals_[i].start()
+        pairs[i].start()
+    rep_local, rep_first, rep_second = [], [], []
+    for i in range(n_rep):
+        mine = all_rows[i].at[rep]
+        theirs = all_rows[i].at[(1 - chip) * 2 + core]
+        rep_local.append(pltpu.make_async_copy(own_rows[i], mine, local_sems.at[n + i]))
+        rep_first.append(remote(own_rows[i], mine, rep_send.at[i, 0], rep_recv.at[i, 0], far))
+        rep_second.append(remote(own_rows[i], mine, rep_send.at[i, 1], rep_recv.at[i, 1], near))
+        rep_second.append(remote(theirs, theirs, rep_send.at[i, 2], rep_recv.at[i, 2], near))
+        rep_local[i].start()
+        rep_first[i].start()
+        rep_second[2 * i].start()
+    for i in range(n):
+        locals_[i].wait()
+        pairs[i].wait_recv()
+        small_rings[i].start()
+    for i in range(n):
+        small_rings[i].forward()
+    for i in range(n):
+        small_rings[i].finish()
+        large_rings[i].start()
+    for i in range(n_rep):
+        rep_first[i].wait_recv()
+        rep_second[2 * i + 1].start()
+    for i in range(n):
+        large_rings[i].forward()
+    swaps = []
+    for i in range(n):
+        large_rings[i].finish()
+        if split[i]:
+            half = wholes[i].at[core]
+            swaps.append(remote(half, half, rep_send.at[n_rep, 0], rep_recv.at[n_rep, 0], near))
+            swaps[-1].start()
+    for i in range(n):
+        pairs[i].wait_send()
+        small_rings[i].drain()
+        large_rings[i].drain()
+    for i in range(n_rep):
+        rep_local[i].wait()
+        rep_first[i].wait_send()
+        for copy in rep_second[2 * i : 2 * i + 2]:
+            copy.wait()
+    for copy in swaps:
+        copy.wait()
+
+
+def gather_weights(blocks, first_x, split, rows):
+    n, n_rep = len(blocks), len(rows)
+    shapes = [
+        jax.ShapeDtypeStruct(((2,) if split[i] else ()) + (4, 4, 2) + blocks[i].shape, blocks[i].dtype)
+        for i in range(n)
+    ] + [jax.ShapeDtypeStruct((REP,) + value.shape, value.dtype) for value in rows]
+    anywhere = pl.BlockSpec(memory_space=pl.ANY)
+    dma = pltpu.SemaphoreType.DMA
+    results = pl.pallas_call(
+        lambda *refs: gather_kernel(first_x, split, n_rep, *refs),
+        name="gather_weights",
+        in_specs=[anywhere] * (n + n_rep),
+        out_specs=[anywhere] * (n + n_rep),
+        out_shape=shapes,
+        scratch_shapes=[
+            dma((n + n_rep,)),
+            dma((n,)),
+            dma((n,)),
+            dma((n, 2, 4)),
+            dma((n, 2, 4)),
+            dma((n_rep + 1, 3)),
+            dma((n_rep + 1, 3)),
+        ],
+        compiler_params=pltpu.CompilerParams(collective_id=0, has_side_effects=True),
+        cost_estimate=estimate(0, 64 << 20, 0),
+    )(*blocks, *rows)
+    return results[:n], results[n:]
+
+
 def norm_parts(values):
     return lax.rsqrt(jnp.mean(values * values, axis=-1, keepdims=True) + epsilon)
 
@@ -444,21 +634,40 @@
     )
     small = jnp.concatenate([self_gain, cross_gain, feed_gain, bias_table[0], jnp.zeros((16,), bf16)])
     small = jnp.broadcast_to(small[None], (8, 128))
-    small = gather_shard(small)[:, 0]
-    w_qkv = gather_shard(qkv_block).reshape(D, QW + 2 * KW)
     down_padded = jnp.pad(down_weight, ((0, 8), (0, 0)))
     rows_piece = jnp.concatenate([piece(out_weight, 8), piece(cross_out, 8), piece(down_padded, 24)], axis=0)
     rows_piece = lax.ppermute(rows_piece, ("rep", "shard"), spread_rows)
     ckv_block = jnp.stack(
         [cross_key.reshape(-1, REP, KW), cross_value.reshape(-1, REP, KW)], axis=2
     ).reshape(-1, 2 * REP * KW)
-    w_ckv = gather_shard(ckv_block).reshape(D, 2 * REP * KW)
-    w_out = gather_shard(rows_piece[0:8]).reshape(QW, D)
-    w_cq = gather_shard(columns(cross_query, QW)).reshape(D, QW)
-    w_cout = gather_shard(rows_piece[8:16]).reshape(QW, D)
-    w_gate = gather_shard(columns(gate_weight, OWN_FF)).reshape(D, OWN_FF)
-    w_up = gather_shard(columns(up_weight, OWN_FF)).reshape(D, OWN_FF)
-    w_down = gather_shard(rows_piece[16:40]).reshape(8, 96, D)[:, :88].reshape(OWN_FF, D)
+    ckv_block = lax.dynamic_slice_in_dim(ckv_block, rep % 2 * REP * KW, REP * KW, 1)
+    own_tokens = tokens.reshape(own, D)
+    own_cotangent = out_cotangent.reshape(own, D)
+    blocks = [
+        qkv_block,
+        small,
+        rows_piece[0:8],
+        ckv_block,
+        columns(cross_query, QW),
+        rows_piece[8:16],
+        columns(gate_weight, OWN_FF),
+        columns(up_weight, OWN_FF),
+        rows_piece[16:40],
+    ]
+    first_x = [True, False, False, True, True, False, True, False, False]
+    split = [False, False, False, True, False, False, False, False, False]
+    (w_qkv, small, w_out, w_ckv, w_cq, w_cout, w_gate, w_up, w_down), (all_tokens, all_grad) = gather_weights(
+        blocks, first_x, split, [own_tokens, own_cotangent]
+    )
+    w_qkv = w_qkv.reshape(D, QW + 2 * KW)
+    small = small.reshape(SHARDS, 8, 128)[:, 0]
+    w_out = w_out.reshape(QW, D)
+    w_ckv = w_ckv.reshape(2, D, REP * KW)
+    w_cq = w_cq.reshape(D, QW)
+    w_cout = w_cout.reshape(QW, D)
+    w_gate = w_gate.reshape(D, OWN_FF)
+    w_up = w_up.reshape(D, OWN_FF)
+    w_down = w_down.reshape(8, 96, D)[:, :88].reshape(OWN_FF, D)
     self_factor = small[:, 0:32].reshape(D).astype(f32)
     cross_factor = small[:, 32:64].reshape(D).astype(f32)
     feed_factor = small[:, 64:96].reshape(D).astype(f32)
@@ -477,16 +686,17 @@
     curve = left_contract(own_table, hot)
     curve = jnp.pad(curve, ((0, 4), (0, 0)))
 
-    own_tokens = tokens.reshape(own, D)
-    own_cotangent = out_cotangent.reshape(own, D)
-    all_tokens = gather_rep(own_tokens).reshape(REP * own, D).astype(f32)
-    all_grad = gather_rep(own_cotangent).reshape(REP * own, D)
+    all_tokens = all_tokens.reshape(REP * own, D).astype(f32)
+    all_grad = all_grad.reshape(REP * own, D)
 
     normed = (all_tokens * norm_parts(all_tokens) * self_factor).astype(bf16)
     qkv = matmul(normed, w_qkv).astype(bf16).reshape(REP, MICRO, ROWS, QW + 2 * KW)
     enc = encoded.reshape(enc_rows, D)
     ckv = jnp.stack(
-        [matmul(enc, w_ckv[:, 2 * KW * r : 2 * KW * (r + 1)]).astype(bf16) for r in range(REP)]
+        [
+            matmul(enc, w_ckv[r // 2, :, 2 * KW * (r % 2) : 2 * KW * (r % 2 + 1)]).astype(bf16)
+            for r in range(REP)
+        ]
     )
     kv = lax.all_to_all(ckv, "rep", 0, 0, tiled=True)
     kv = kv.reshape(REP, MICRO, DOCS, ENC // REP, 2 * KW)
@@ -539,9 +749,9 @@
 
     ckv_grad = lax.all_to_all(kv_grad.reshape(REP, enc_rows, 2 * KW), "rep", 0, 0, tiled=True)
     ckv_grad = jnp.concatenate([ckv_grad[r] for r in range(REP)], axis=1)
-    encoder_grad = right_contract(ckv_grad, w_ckv)
     core = rep % 2
     half = REP * KW
+    encoder_grad = right_contract(ckv_grad[:, :half], w_ckv[0]) + right_contract(ckv_grad[:, half:], w_ckv[1])
     ckv_part = left_contract(enc, ckv_grad)
     given = lax.dynamic_slice_in_dim(ckv_part, (1 - core) * half, half, 1).astype(bf16)
     kept = lax.dynamic_slice_in_dim(ckv_part, core * half, half, 1)

time: 688 us -> 583 us (0.85)
  waiting for transfers between devices: 219 us -> 141 us
  Pallas kernels: 52.3 us -> 110 us
  starting transfers between devices: 175 us -> 121 us
  matrix products: 60 us -> 45.2 us
  local copies, waits for them, and re-layouts: 89.5 us -> 81 us
    pallas_call x0 -> x1, Pallas kernels: none -> 58.2 us  [gather_weights(): pl.pallas_call(lambda *refs: gather_kernel(first_x, split, n_rep, *refs),...]
    all_to_all x9 -> x0, starting transfers between devices: 57.6 us -> none  [gather_shard(): lax.all_to_all(jnp.broadcast_to(block[None], (SHARDS,) + block.shape), 's...]
    all_to_all x9 -> x0, waiting for transfers between devices: 49.2 us -> none  [gather_shard(): lax.all_to_all(jnp.broadcast_to(block[None], (SHARDS,) + block.shape), 's...]
    ppermute x19 -> x17, waiting for transfers between devices: 104 us -> 81 us  [other_chip(): return lax.ppermute(value, 'rep', swap_chip)]
    broadcast_in_dim x9 -> x1, local copies, waits for them, and re-layouts: 11 us -> 0.58 us  [local(): small = jnp.broadcast_to(small[None], (8, 128))]
    all_to_all x8, waiting for transfers between devices: 52.8 us -> 43.2 us  [scatter_shard(): sent = lax.all_to_all(parts.astype(bf16), 'shard', 0, 0, tiled=True)]
    select_n x31 -> x26, other arithmetic: 27.6 us -> 18 us  [in_order(): jnp.where(flag == 0, jnp.stack([own, other], axis), jnp.stack([other, own...]
    dot_general x11, matrix products: 24.2 us -> 15.2 us  [matmul(): return jnp.dot(left, right, preferred_element_type=f32)]
  transfers between devices with their start and end apart: 61 -> 48, of which waited for: 31 -> 23; matrix products, arithmetic and copies ran while one was open for 29% -> 25% of each run, Pallas kernels for 8% -> 2%
where the time goes in v2:
time: 583 us; the launch traced here: 572 us
  waiting for transfers between devices  141 us (24%)
  starting transfers between devices  121 us (21%)
  Pallas kernels  110 us (19%)
  local copies, waits for them, and re-layouts  81 us (14%)
  other arithmetic  71.2 us (12%)
  matrix products  45.2 us (8%)
    ppermute x17, waiting for transfers between devices, other_chip(): return lax.ppermute(value, 'rep', swap_chip)  81 us
    pallas_call x1, Pallas kernels, gather_weights(): pl.pallas_call(lambda *refs: gather_kernel(first_x, split, n_rep, *refs),...  58.2 us
    all_to_all x8, starting transfers between devices, scatter_shard(): sent = lax.all_to_all(parts.astype(bf16), 'shard', 0, 0, tiled=True)  46.6 us
    all_to_all x8, waiting for transfers between devices, scatter_shard(): sent = lax.all_to_all(parts.astype(bf16), 'shard', 0, 0, tiled=True)  43.2 us
    ppermute x18, starting transfers between devices, other_core(): return lax.ppermute(value, 'rep', swap_core)  29.7 us
    pallas_call x1, Pallas kernels, cross_backward(): pl.pallas_call(cross_backward_kernel, name='cross_backward', grid_spec=pl...  23.4 us
    select_n x26, other arithmetic, in_order(): jnp.where(flag == 0, jnp.stack([own, other], axis), jnp.stack([other, own...  18 us
    unnamed x135, local copies, waits for them, and re-layouts  17.9 us
  transfers between devices with their start and end apart: 48, of which 23 were waited for; matrix products, arithmetic and copies ran while one was open for 25% of the time, Pallas kernels for 2%

profile of v2, /device:TPU:1, one launch (start us, length us, event | category | flops | bytes accessed | tf_op | source)
XLA Modules:
  0.0 571.9 jit_solution(16106651365930158180)
XLA Ops:
  2.4 6.9 %collective-permute-start = (bf16[40,1024]{1,0:T(8,128)(2,1)S(1)}, bf16[40,1024]{1,0:T(8,128)(2,1)S(1)}, u32[]{:S(2)}, u32[]{:S(2)}) collective-permute-start(bf16[40,1024]{1,0:T(8,128)(2,1)S(1)} %pad_maximum_fusion.3), channel_id=1, source_target_pairs={{0,0},{1,4},{2,8},{3,12},{4,16},{5,20},{6,24},{7,28},{8,32},{9,36}... | collective-permute-start | bytes 245768 | tf_op jit(solution)/shard_map/ppermute | solution.py:639
  19.6 2.8 concatenate.174
  24.9 58.2 %gather_weights.1 = (bf16[4,4,2,32,512]{4,3,2,1,0:T(8,128)(2,1)}, bf16[4,4,2,8,128]{4,3,2,1,0:T(8,128)(2,1)}, bf16[4,4,2,8,1024]{4,3,2,1,0:T(8,128)(2,1)}, bf16[...) custom-call(bf16[32,512]{1,0:T(8,128)(2,1)} %pad_maximum_fusion.8.re, ...), custom_call_target="tpu_custom_call" | custom-call | bytes 67108864 | tf_op jit(solution)/shard_map/gather_weights/pallas_call | solution.py:567
  88.4 4.9 self_forward.1
  102.7 2.9 pad_maximum_fusion
  105.6 5.8 %all-to-all-start = ((bf16[4,1024,256]{1,2,0:T(8,128)(2,1)}), bf16[4,1024,256]{1,2,0:T(8,128)(2,1)}, u32[]{:S(2)}, u32[]{:S(2)}) async-start(bf16[4,1024,256]{1,2,0:T(8,128)(2,1)} %pad_maximum_fusion), calls=%async_computation | async-start | bytes 4194304 | tf_op jit(solution)/shard_map/all_to_all | solution.py:701
  116.6 25.2 %collective-permute-done.3 = bf16[128,1024]{1,0:T(8,128)(2,1)S(1)} collective-permute-done((bf16[128,1024]{1,0:T(8,128)(2,1)}, bf16[128,1024]{1,0:T(8,128)(2,1)S(1)}, u32[]{:S(2)}, u32[]{:S(2)}) %collective-permute-start.3) | collective-permute-done | bytes 262176 | tf_op jit(solution)/shard_map/ppermute | solution.py:357
  146.3 3.9 copy.141
  151.8 14.4 %cross_forward.1 = bf16[4,2,64,256]{3,2,1,0:T(8,128)(2,1)S(1)} custom-call(s32[8]{0:T(128)S(1)} %reshape_squeeze.9.block_ref, s32[8]{0:T(128)S(1)} %multiply_minimum_fusion.start_ref, bf16[4,2,64,256]{3,2,1,0:T(8,128)(2,1)S(1)} %bitcast.486, bf16[4,2,4,128,256]{4,3,2,1,0:T(8,128)(2,1)S(1)} %bitcast.475, ...), custom_call_target="tpu_custom_call" | custom-call | flops 603979776 | bytes 3145728 | tf_op jit(solution)/shard_map/cross_forward/pallas_call | solution.py:305
  170.9 7.7 %collective-permute-done.6 = bf16[128,1024]{1,0:T(8,128)(2,1)} collective-permute-done((bf16[128,1024]{1,0:T(8,128)(2,1)}, bf16[128,1024]{1,0:T(8,128)(2,1)}, u32[]{:S(2)}, u32[]{:S(2)}) %collective-permute-start.6) | collective-permute-done | bytes 262176 | tf_op jit(solution)/shard_map/ppermute | solution.py:357
  183.0 5.5 collective-permute-done.7
  190.5 2.1 collective-permute-start.8
  193.2 2.6 slice.267
  199.6 2.3 copy.164
  201.9 2.8 fusion.88
  204.8 2.1 fusion.26
  206.9 3.1 fusion.17
  210.9 2.2 convolution_convert_fusion.1
  213.0 7.9 %all-to-all-start.9 = ((bf16[32,32,704]{2,1,0:T(8,128)(2,1)}), bf16[32,32,704]{2,1,0:T(8,128)(2,1)}, u32[]{:S(2)}, u32[]{:S(2)}) async-start(bf16[32,32,704]{2,1,0:T(8,128)(2,1)} %convolution_convert_fusion.1), calls=%async_computation.9 | async-start | bytes 3145728 | tf_op jit(solution)/shard_map/all_to_all | solution.py:394
  220.9 2.5 fusion.10
  223.5 2.3 copy.159
  226.6 2.8 fusion.89
  233.0 2.8 dot_general.139
  235.8 3.7 convolution_convert_fusion
  239.5 5.8 %all-to-all-done.9 = bf16[32,32,704]{2,1,0:T(8,128)(2,1)} async-done(((bf16[32,32,704]{2,1,0:T(8,128)(2,1)}), bf16[32,32,704]{2,1,0:T(8,128)(2,1)}, u32[]{:S(2)}, u32[]{:S(2)}) %all-to-all-start.9) | async-done | bytes 1441824 | tf_op jit(solution)/shard_map/all_to_all | solution.py:394
  245.3 4.7 all-to-all-start.10
  250.0 2.7 fusion.41
  261.8 11.1 %all-to-all-done.10 = bf16[32,32,704]{2,1,0:T(8,128)(2,1)} async-done(((bf16[32,32,704]{2,1,0:T(8,128)(2,1)}), bf16[32,32,704]{2,1,0:T(8,128)(2,1)}, u32[]{:S(2)}, u32[]{:S(2)}) %all-to-all-start.10) | async-done | bytes 1441824 | tf_op jit(solution)/shard_map/all_to_all | solution.py:394
  272.9 4.9 all-to-all-start.6
  280.5 2.7 fusion.82
  283.2 2.0 collective-permute-start.13
  287.6 2.3 copy.162
  290.0 12.6 %collective-permute-done.13 = bf16[128,1024]{1,0:T(8,128)(2,1)} collective-permute-done((bf16[128,1024]{1,0:T(8,128)(2,1)S(1)}, bf16[128,1024]{1,0:T(8,128)(2,1)}, u32[]{:S(2)}, u32[]{:S(2)}) %collective-permute-start.13) | collective-permute-done | bytes 262176 | tf_op jit(solution)/shard_map/ppermute | solution.py:357
  302.6 2.0 maximum_select_fusion.8
  307.0 2.1 collective-permute-start.33
  309.1 2.0 maximum_select_fusion.7
  313.8 2.0 collective-permute-done.35
  319.3 2.3 reduce.9
  328.7 23.4 %cross_backward.1 = (bf16[4,2,64,256]{3,2,1,0:T(8,128)(2,1)S(1)}, bf16[4,2,4,128,256]{4,3,2,1,0:T(8,128)(2,1)S(1)}) custom-call(s32[8]{0:T(128)S(1)} %reshape_squeeze.9.block_ref, s32[8]{0:T(128)S(1)} %multiply_minimum_fusion.start_ref, bf16[4,2,64,256]{3,2,1,0:T(8,128)(2,1)S(1)} %bitcast.487, bf16[4,2,4,128,256]{4,3,2,1,0:T(8,128)(2,1)S(1)} %bitcast.476, ...), custom_call_target="tpu_custom_call" | custom-call | flops 1509949440 | bytes 6291456 | tf_op jit(solution)/shard_map/cross_backward/pallas_call | solution.py:322
  357.4 7.6 %all-to-all-start.7 = ((bf16[32,32,256]{2,1,0:T(8,128)(2,1)}), bf16[32,32,256]{2,1,0:T(8,128)(2,1)S(1)}, u32[]{:S(2)}, u32[]{:S(2)}) async-start(bf16[32,32,256]{2,1,0:T(8,128)(2,1)} %convolution_convert_fusion.4), calls=%async_computation.7 | async-start | bytes 1048576 | tf_op jit(solution)/shard_map/all_to_all | solution.py:394
  365.0 2.5 convolution_convert_fusion.5
  367.5 2.6 bitcast_add_fusion.2
  370.1 7.3 %all-to-all-done.7 = bf16[32,32,256]{2,1,0:T(8,128)(2,1)S(1)} async-done(((bf16[32,32,256]{2,1,0:T(8,128)(2,1)}), bf16[32,32,256]{2,1,0:T(8,128)(2,1)S(1)}, u32[]{:S(2)}, u32[]{:S(2)}) %all-to-all-start.7) | async-done | bytes 524320 | tf_op jit(solution)/shard_map/all_to_all | solution.py:394
  377.4 4.6 all-to-all-start.5
  393.4 7.7 %all-to-all-start.1 = ((bf16[4,1024,256]{2,1,0:T(8,128)(2,1)}), bf16[4,1024,256]{2,1,0:T(8,128)(2,1)}, u32[]{:S(2)}, u32[]{:S(2)}) async-start(bf16[4,1024,256]{2,1,0:T(8,128)(2,1)} %bitcast.477), calls=%async_computation.1 | async-start | bytes 4194304 | tf_op jit(solution)/shard_map/all_to_all | solution.py:750
  403.6 2.3 fusion.81
  408.9 22.7 %collective-permute-done.17 = bf16[128,1024]{1,0:T(8,128)(2,1)S(1)} collective-permute-done((bf16[128,1024]{1,0:T(8,128)(2,1)S(1)}, bf16[128,1024]{1,0:T(8,128)(2,1)S(1)}, u32[]{:S(2)}, u32[]{:S(2)}) %collective-permute-start.17) | collective-permute-done | bytes 262176 | tf_op jit(solution)/shard_map/ppermute | solution.py:357
  437.8 9.5 %self_backward.1 = (bf16[4,2,64,512]{3,2,1,0:T(8,128)(2,1)S(1)}, f32[8,256]{1,0:T(8,128)S(1)}) custom-call(bf16[4,2,64,512]{3,2,1,0:T(8,128)(2,1)S(1)} %bitcast.485, bf16[4,2,64,256]{3,2,1,0:T(8,128)(2,1)S(1)} %bitcast.489, s32[2,256,1]{2,1,0:T(8,128)S(1)} %broadcast_in_dim_squeeze.4.seg_col_ref.seg_ref, s32[2,1,256]{2,1,0:T(1,128)S(1)} %copy-done.6, ...), custom_call_target="tpu_custom_call" | custom-call | flops 335544320 | bytes 3145728 | tf_op jit(solution)/shard_map/self_backward/pallas_call | solution.py:264
  452.0 8.3 %all-to-all-start.4 = ((bf16[32,8,1024]{2,1,0:T(8,128)(2,1)}), bf16[32,8,1024]{2,1,0:T(8,128)(2,1)}, u32[]{:S(2)}, u32[]{:S(2)}) async-start(bf16[32,8,1024]{2,1,0:T(8,128)(2,1)} %convolution_convert_fusion.6), calls=%async_computation.4 | async-start | bytes 1048576 | tf_op jit(solution)/shard_map/all_to_all | solution.py:394
  463.4 2.5 fusion
  469.6 3.3 convolution_add_fusion
  476.6 3.6 collective-permute-start.25
  480.7 7.2 %collective-permute-done.25 = bf16[40,1024]{1,0:T(8,128)(2,1)S(1)} collective-permute-done((bf16[40,1024]{1,0:T(8,128)(2,1)S(1)}, bf16[40,1024]{1,0:T(8,128)(2,1)S(1)}, u32[]{:S(2)}, u32[]{:S(2)}) %collective-permute-start.25) | collective-permute-done | bytes 81952 | tf_op jit(solution)/shard_map/ppermute | solution.py:796
  490.1 8.3 %all-to-all-start.2 = ((f32[32,8,128]{2,1,0:T(8,128)}), f32[32,8,128]{2,1,0:T(8,128)}, u32[]{:S(2)}, u32[]{:S(2)}) async-start(f32[32,8,128]{2,1,0:T(8,128)} %broadcast_in_dim.5), calls=%async_computation.2 | async-start | bytes 262144 | tf_op jit(solution)/shard_map/all_to_all | solution.py:784
  499.1 3.1 collective-permute-start.27
  502.2 5.0 all-to-all-done.2
  507.2 4.7 all-to-all-start.3
  511.9 2.0 fusion.45
  518.5 7.8 %collective-permute-start.22 = (f32[8,128]{1,0:T(8,128)S(1)}, f32[8,128]{1,0:T(8,128)S(1)}, u32[]{:S(2)}, u32[]{:S(2)}) collective-permute-start(f32[8,128]{1,0:T(8,128)S(1)} %add.266), channel_id=1, source_target_pairs={{0,32},{32,0},{64,96},{96,64},{1,33},{33,1},{65,97},{97,65},{2,34}... | collective-permute-start | bytes 12296 | tf_op jit(solution)/shard_map/ppermute | solution.py:361
  532.0 5.3 collective-permute-start.24
  537.3 3.3 fusion.8
  540.5 3.9 all-to-all-start.8
  545.3 18.1 %all-to-all-done.8 = bf16[32,32,512]{2,1,0:T(8,128)(2,1)S(1)} async-done(((bf16[32,32,512]{2,1,0:T(8,128)(2,1)}), bf16[32,32,512]{2,1,0:T(8,128)(2,1)S(1)}, u32[]{:S(2)}, u32[]{:S(2)}) %all-to-all-start.8) | async-done | bytes 1048608 | tf_op jit(solution)/shard_map/all_to_all | solution.py:394
  566.4 2.3 collective-permute-start.32
  (372 shorter events, 154.3 us)
Async XLA Ops:
  0.7 93.8 %copy-start = (bf16[2,1,4,128,1024]{4,3,2,1,0:T(8,128)(2,1)S(1)}, bf16[2,1,4,128,1024]{4,3,2,1,0:T(8,128)(2,1)}, u32[]{:S(2)}) copy-start(bf16[2,1,4,128,1024]{4,3,2,1,0:T(8,128)(2,1)} %param.23) | copy-start | bytes 6291460
  2.4 20.7 %collective-permute-start = (bf16[40,1024]{1,0:T(8,128)(2,1)S(1)}, bf16[40,1024]{1,0:T(8,128)(2,1)S(1)}, u32[]{:S(2)}, u32[]{:S(2)}) collective-permute-start(bf16[40,1024]{1,0:T(8,128)(2,1)S(1)} %pad_maximum_fusion.3), channel_id=1, source_target_pairs={{0,0},{1,4},{2,8},{3,12},{4,16},{5,20},{6,24},{7,28},{8,32},{9,36}... | collective-permute-start | bytes 245768 | tf_op jit(solution)/shard_map/ppermute | solution.py:639
  23.1 65.0 %copy-start.54 = (s32[256]{0:T(256)}, s32[256]{0:T(256)S(1)}, u32[]{:S(2)}) copy-start(s32[256]{0:T(256)S(1)} %pad_add_fusion) | copy-start | bytes 3076
  93.8 5.0 collective-permute-start.1
  100.7 10.6 %collective-permute-start.2 = (bf16[128,1024]{1,0:T(8,128)(2,1)}, bf16[128,1024]{1,0:T(8,128)(2,1)}, u32[]{:S(2)}, u32[]{:S(2)}) collective-permute-start(bf16[128,1024]{1,0:T(8,128)(2,1)} %fusion.59), channel_id=1, source_target_pairs={{0,64},{32,96},{64,0},{96,32},{1,65},{33,97},{65,1},{97,33},{2,66}... | collective-permute-start | bytes 786440 | tf_op jit(solution)/shard_map/ppermute | solution.py:357
  105.6 40.7 %all-to-all-start = ((bf16[4,1024,256]{1,2,0:T(8,128)(2,1)}), bf16[4,1024,256]{1,2,0:T(8,128)(2,1)}, u32[]{:S(2)}, u32[]{:S(2)}) async-start(bf16[4,1024,256]{1,2,0:T(8,128)(2,1)} %pad_maximum_fusion), calls=%async_computation | async-start | bytes 4194304 | tf_op jit(solution)/shard_map/all_to_all | solution.py:701
  112.7 30.6 %copy-start.7 = (f32[128,1024]{1,0:T(8,128)}, f32[128,1024]{1,0:T(8,128)S(1)}, u32[]{:S(2)}) copy-start(f32[128,1024]{1,0:T(8,128)S(1)} %get-tuple-element.135) | copy-start | bytes 1572868
  113.6 28.2 %collective-permute-start.3 = (bf16[128,1024]{1,0:T(8,128)(2,1)}, bf16[128,1024]{1,0:T(8,128)(2,1)S(1)}, u32[]{:S(2)}, u32[]{:S(2)}) collective-permute-start(bf16[128,1024]{1,0:T(8,128)(2,1)} %multiply_convert_fusion.4), channel_id=1, source_target_pairs={{0,64},{32,96},{64,0},{96,32},{1,65},{33,97},{65,1},{97,33},{2,66}... | collective-permute-start | bytes 786440 | tf_op jit(solution)/shard_map/ppermute | solution.py:357
  141.9 2.7 collective-permute-start.4
  151.8 14.4 %copy-start.49 = (bf16[4,4,2,8,1024]{4,3,2,1,0:T(8,128)(2,1)S(1)}, bf16[4,4,2,8,1024]{4,3,2,1,0:T(8,128)(2,1)}, u32[]{:S(2)}) copy-start(bf16[4,4,2,8,1024]{4,3,2,1,0:T(8,128)(2,1)} %get-tuple-element.39) | copy-start | bytes 1572868
  166.8 2.0 collective-permute-start.5
  170.0 11.7 %copy-start.12 = (bf16[2,1,64,1024]{3,2,1,0:T(8,128)(2,1)S(1)}, bf16[2,1,64,1024]{3,2,1,0:T(8,128)(2,1)}, u32[]{:S(2)}) copy-start(bf16[2,1,64,1024]{3,2,1,0:T(8,128)(2,1)} %param.21) | copy-start | bytes 786436
  170.8 7.8 %collective-permute-start.6 = (bf16[128,1024]{1,0:T(8,128)(2,1)}, bf16[128,1024]{1,0:T(8,128)(2,1)}, u32[]{:S(2)}, u32[]{:S(2)}) collective-permute-start(bf16[128,1024]{1,0:T(8,128)(2,1)} %fusion.60), channel_id=1, source_target_pairs={{0,64},{32,96},{64,0},{96,32},{1,65},{33,97},{65,1},{97,33},{2,66}... | collective-permute-start | bytes 786440 | tf_op jit(solution)/shard_map/ppermute | solution.py:357
  181.7 6.9 %collective-permute-start.7 = (bf16[128,1024]{1,0:T(8,128)(2,1)}, bf16[128,1024]{1,0:T(8,128)(2,1)}, u32[]{:S(2)}, u32[]{:S(2)}) collective-permute-start(bf16[128,1024]{1,0:T(8,128)(2,1)} %multiply_convert_fusion.3), channel_id=1, source_target_pairs={{0,64},{32,96},{64,0},{96,32},{1,65},{33,97},{65,1},{97,33},{2,66}... | collective-permute-start | bytes 786440 | tf_op jit(solution)/shard_map/ppermute | solution.py:357
  190.5 6.6 %collective-permute-start.8 = (bf16[2,128,1024]{2,1,0:T(8,128)(2,1)}, bf16[2,128,1024]{2,1,0:T(8,128)(2,1)}, u32[]{:S(2)}, u32[]{:S(2)}) collective-permute-start(bf16[2,128,1024]{2,1,0:T(8,128)(2,1)} %maximum_select_fusion.6), channel_id=1, source_target_pairs={{0,32},{32,0},{64,96},{96,64},{1,33},{33,1},{65,97},{97,65},{2,34}... | collective-permute-start | bytes 1572872 | tf_op jit(solution)/shard_map/ppermute | solution.py:361
  213.0 32.2 %all-to-all-start.9 = ((bf16[32,32,704]{2,1,0:T(8,128)(2,1)}), bf16[32,32,704]{2,1,0:T(8,128)(2,1)}, u32[]{:S(2)}, u32[]{:S(2)}) async-start(bf16[32,32,704]{2,1,0:T(8,128)(2,1)} %convolution_convert_fusion.1), calls=%async_computation.9 | async-start | bytes 3145728 | tf_op jit(solution)/shard_map/all_to_all | solution.py:394
  232.8 23.5 %collective-permute-start.11 = (bf16[2,128,1024]{2,1,0:T(8,128)(2,1)}, bf16[2,128,1024]{2,1,0:T(8,128)(2,1)}, u32[]{:S(2)}, u32[]{:S(2)}) collective-permute-start(bf16[2,128,1024]{2,1,0:T(8,128)(2,1)} %fusion.50), channel_id=1, source_target_pairs={{0,32},{32,0},{64,96},{96,64},{1,33},{33,1},{65,97},{97,65},{2,34}... | collective-permute-start | bytes 1572872 | tf_op jit(solution)/shard_map/ppermute | solution.py:361
  245.3 27.7 %all-to-all-start.10 = ((bf16[32,32,704]{2,1,0:T(8,128)(2,1)}), bf16[32,32,704]{2,1,0:T(8,128)(2,1)}, u32[]{:S(2)}, u32[]{:S(2)}) async-start(bf16[32,32,704]{2,1,0:T(8,128)(2,1)} %convolution_convert_fusion), calls=%async_computation.10 | async-start | bytes 3145728 | tf_op jit(solution)/shard_map/all_to_all | solution.py:394
  252.8 6.2 %collective-permute-start.9 = (bf16[2,128,1024]{2,1,0:T(8,128)(2,1)S(1)}, bf16[2,128,1024]{2,1,0:T(8,128)(2,1)S(1)}, u32[]{:S(2)}, u32[]{:S(2)}) collective-permute-start(bf16[2,128,1024]{2,1,0:T(8,128)(2,1)S(1)} %fusion.52), channel_id=1, source_target_pairs={{0,32},{32,0},{64,96},{96,64},{1,33},{33,1},{65,97},{97,65},{2,34}... | collective-permute-start | bytes 1572872 | tf_op jit(solution)/shard_map/ppermute | solution.py:361
  259.0 18.8 %collective-permute-start.12 = (bf16[128,1024]{1,0:T(8,128)(2,1)}, bf16[128,1024]{1,0:T(8,128)(2,1)S(1)}, u32[]{:S(2)}, u32[]{:S(2)}) collective-permute-start(bf16[128,1024]{1,0:T(8,128)(2,1)} %fusion.62), channel_id=1, source_target_pairs={{0,64},{32,96},{64,0},{96,32},{1,65},{33,97},{65,1},{97,33},{2,66}... | collective-permute-start | bytes 786440 | tf_op jit(solution)/shard_map/ppermute | solution.py:357
  260.4 20.1 %collective-permute-start.10 = (bf16[128,1024]{1,0:T(8,128)(2,1)}, bf16[128,1024]{1,0:T(8,128)(2,1)}, u32[]{:S(2)}, u32[]{:S(2)}) collective-permute-start(bf16[128,1024]{1,0:T(8,128)(2,1)} %fusion.61), channel_id=1, source_target_pairs={{0,64},{32,96},{64,0},{96,32},{1,65},{33,97},{65,1},{97,33},{2,66}... | collective-permute-start | bytes 786440 | tf_op jit(solution)/shard_map/ppermute | solution.py:357
  272.9 46.4 %all-to-all-start.6 = ((bf16[32,24,1024]{2,1,0:T(8,128)(2,1)}), bf16[32,24,1024]{2,1,0:T(8,128)(2,1)}, u32[]{:S(2)}, u32[]{:S(2)}) async-start(bf16[32,24,1024]{2,1,0:T(8,128)(2,1)} %bitcast.493), calls=%async_computation.6 | async-start | bytes 3145728 | tf_op jit(solution)/shard_map/all_to_all | solution.py:394
  277.8 7.4 %copy-start.31 = (bf16[2,4,4,2,32,512]{5,4,3,2,1,0:T(8,128)(2,1)S(1)}, bf16[2,4,4,2,32,512]{5,4,3,2,1,0:T(8,128)(2,1)}, u32[]{:S(2)}) copy-start(bf16[2,4,4,2,32,512]{5,4,3,2,1,0:T(8,128)(2,1)} %get-tuple-element.38) | copy-start | bytes 6291460
  283.2 19.4 %collective-permute-start.13 = (bf16[128,1024]{1,0:T(8,128)(2,1)S(1)}, bf16[128,1024]{1,0:T(8,128)(2,1)}, u32[]{:S(2)}, u32[]{:S(2)}) collective-permute-start(bf16[128,1024]{1,0:T(8,128)(2,1)S(1)} %get-tuple-element.130), channel_id=1, source_target_pairs={{0,64},{32,96},{64,0},{96,32},{1,65},{33,97},{65,1},{97,33},{2,66}... | collective-permute-start | bytes 786440 | tf_op jit(solution)/shard_map/ppermute | solution.py:357
  304.6 20.7 %collective-permute-start.14 = (bf16[2,128,1024]{2,1,0:T(8,128)(2,1)}, bf16[2,128,1024]{2,1,0:T(8,128)(2,1)}, u32[]{:S(2)}, u32[]{:S(2)}) collective-permute-start(bf16[2,128,1024]{2,1,0:T(8,128)(2,1)} %maximum_select_fusion.8), channel_id=1, source_target_pairs={{0,32},{32,0},{64,96},{96,64},{1,33},{33,1},{65,97},{97,65},{2,34}... | collective-permute-start | bytes 1572872 | tf_op jit(solution)/shard_map/ppermute | solution.py:361
  307.0 5.8 %collective-permute-start.33 = (bf16[32,704]{1,0:T(8,128)(2,1)S(1)}, bf16[32,704]{1,0:T(8,128)(2,1)S(1)}, u32[]{:S(2)}, u32[]{:S(2)}) collective-permute-start(bf16[32,704]{1,0:T(8,128)(2,1)S(1)} %reduce_sum.213), channel_id=1, source_target_pairs={{0,64},{32,96},{64,0},{96,32},{1,65},{33,97},{65,1},{97,33},{2,66}... | collective-permute-start | bytes 135176 | tf_op jit(solution)/shard_map/ppermute | solution.py:357
  312.7 3.0 collective-permute-start.35
  313.5 8.2 %collective-permute-start.34 = (bf16[2,32,704]{2,1,0:T(8,128)(2,1)}, bf16[2,32,704]{2,1,0:T(8,128)(2,1)}, u32[]{:S(2)}, u32[]{:S(2)}) collective-permute-start(bf16[2,32,704]{2,1,0:T(8,128)(2,1)} %maximum_select_fusion.17), channel_id=1, source_target_pairs={{0,32},{32,0},{64,96},{96,64},{1,33},{33,1},{65,97},{97,65},{2,34}... | collective-permute-start | bytes 270344 | tf_op jit(solution)/shard_map/ppermute | solution.py:361
  316.4 7.1 %collective-permute-start.36 = (bf16[2,32,704]{2,1,0:T(8,128)(2,1)}, bf16[2,32,704]{2,1,0:T(8,128)(2,1)}, u32[]{:S(2)}, u32[]{:S(2)}) collective-permute-start(bf16[2,32,704]{2,1,0:T(8,128)(2,1)} %maximum_select_fusion.18), channel_id=1, source_target_pairs={{0,32},{32,0},{64,96},{96,64},{1,33},{33,1},{65,97},{97,65},{2,34}... | collective-permute-start | bytes 270344 | tf_op jit(solution)/shard_map/ppermute | solution.py:361
  318.6 6.7 %copy-start.29 = (bf16[2,1,128,1024]{3,2,0,1:T(8,128)(2,1)S(1)}, bf16[2,1,128,1024]{3,2,0,1:T(8,128)(2,1)}, u32[]{:S(2)}) copy-start(bf16[2,1,128,1024]{3,2,0,1:T(8,128)(2,1)} %maximum_select_fusion.7) | copy-start | bytes 1572868
  328.7 24.8 %copy-start.48 = (bf16[4,4,2,32,256]{4,3,2,1,0:T(8,128)(2,1)S(1)}, bf16[4,4,2,32,256]{4,3,2,1,0:T(8,128)(2,1)}, u32[]{:S(2)}) copy-start(bf16[4,4,2,32,256]{4,3,2,1,0:T(8,128)(2,1)} %get-tuple-element.37) | copy-start | bytes 1572868
  355.3 9.7 %copy-start.37 = (bf16[256,512]{1,0:T(8,128)(2,1)S(1)}, bf16[256,512]{1,0:T(8,128)(2,1)}, u32[]{:S(2)}) copy-start(bf16[256,512]{1,0:T(8,128)(2,1)} %copy.161) | copy-start | bytes 786436
  356.2 11.3 %collective-permute-start.15 = (bf16[2,128,1024]{2,1,0:T(8,128)(2,1)}, bf16[2,128,1024]{2,1,0:T(8,128)(2,1)}, u32[]{:S(2)}, u32[]{:S(2)}) collective-permute-start(bf16[2,128,1024]{2,1,0:T(8,128)(2,1)} %fusion.51), channel_id=1, source_target_pairs={{0,32},{32,0},{64,96},{96,64},{1,33},{33,1},{65,97},{97,65},{2,34}... | collective-permute-start | bytes 1572872 | tf_op jit(solution)/shard_map/ppermute | solution.py:361
  357.4 20.0 %all-to-all-start.7 = ((bf16[32,32,256]{2,1,0:T(8,128)(2,1)}), bf16[32,32,256]{2,1,0:T(8,128)(2,1)S(1)}, u32[]{:S(2)}, u32[]{:S(2)}) async-start(bf16[32,32,256]{2,1,0:T(8,128)(2,1)} %convolution_convert_fusion.4), calls=%async_computation.7 | async-start | bytes 1048576 | tf_op jit(solution)/shard_map/all_to_all | solution.py:394
  377.4 16.0 %all-to-all-start.5 = ((bf16[32,8,1024]{2,1,0:T(8,128)(2,1)}), bf16[32,8,1024]{2,1,0:T(8,128)(2,1)}, u32[]{:S(2)}, u32[]{:S(2)}) async-start(bf16[32,8,1024]{2,1,0:T(8,128)(2,1)} %convolution_convert_fusion.5), calls=%async_computation.5 | async-start | bytes 1048576 | tf_op jit(solution)/shard_map/all_to_all | solution.py:394
  383.8 18.4 %collective-permute-start.16 = (bf16[128,1024]{1,0:T(8,128)(2,1)}, bf16[128,1024]{1,0:T(8,128)(2,1)S(1)}, u32[]{:S(2)}, u32[]{:S(2)}) collective-permute-start(bf16[128,1024]{1,0:T(8,128)(2,1)} %fusion.63), channel_id=1, source_target_pairs={{0,64},{32,96},{64,0},{96,32},{1,65},{33,97},{65,1},{97,33},{2,66}... | collective-permute-start | bytes 786440 | tf_op jit(solution)/shard_map/ppermute | solution.py:357
  391.1 16.2 %collective-permute-start.28 = (bf16[32,256]{1,0:T(8,128)(2,1)S(1)}, bf16[32,256]{1,0:T(8,128)(2,1)S(1)}, u32[]{:S(2)}, u32[]{:S(2)}) collective-permute-start(bf16[32,256]{1,0:T(8,128)(2,1)S(1)} %reduce_sum.211), channel_id=1, source_target_pairs={{0,64},{32,96},{64,0},{96,32},{1,65},{33,97},{65,1},{97,33},{2,66}... | collective-permute-start | bytes 49160 | tf_op jit(solution)/shard_map/ppermute | solution.py:357
  393.4 8.8 %copy-start.8 = (f32[128,1024]{1,0:T(8,128)S(1)}, f32[128,1024]{1,0:T(8,128)}, u32[]{:S(2)}) copy-start(f32[128,1024]{1,0:T(8,128)} %copy-done.7) | copy-start | bytes 1572868
  393.4 10.2 %copy-start.59 = (f32[128]{0:T(128)S(1)}, f32[128]{0:T(128)}, u32[]{:S(2)}) copy-start(f32[128]{0:T(128)} %copy-done.58) | copy-start | bytes 1540
  393.4 58.6 %all-to-all-start.1 = ((bf16[4,1024,256]{2,1,0:T(8,128)(2,1)}), bf16[4,1024,256]{2,1,0:T(8,128)(2,1)}, u32[]{:S(2)}, u32[]{:S(2)}) async-start(bf16[4,1024,256]{2,1,0:T(8,128)(2,1)} %bitcast.477), calls=%async_computation.1 | async-start | bytes 4194304 | tf_op jit(solution)/shard_map/all_to_all | solution.py:750
  405.9 25.7 %collective-permute-start.17 = (bf16[128,1024]{1,0:T(8,128)(2,1)S(1)}, bf16[128,1024]{1,0:T(8,128)(2,1)S(1)}, u32[]{:S(2)}, u32[]{:S(2)}) collective-permute-start(bf16[128,1024]{1,0:T(8,128)(2,1)S(1)} %get-tuple-element.128), channel_id=1, source_target_pairs={{0,64},{32,96},{64,0},{96,32},{1,65},{33,97},{65,1},{97,33},{2,66}... | collective-permute-start | bytes 786440 | tf_op jit(solution)/shard_map/ppermute | solution.py:357
  407.3 1.6 collective-permute-start.29
  432.4 2.9 collective-permute-start.18
  436.9 10.4 %copy-start.35 = (bf16[4,4,2,32,512]{4,3,2,1,0:T(8,128)(2,1)S(1)}, bf16[4,4,2,32,512]{4,3,2,1,0:T(8,128)(2,1)}, u32[]{:S(2)}) copy-start(bf16[4,4,2,32,512]{4,3,2,1,0:T(8,128)(2,1)} %get-tuple-element.35) | copy-start | bytes 3145732
  450.3 23.9 %collective-permute-start.19 = (bf16[2,128,1024]{2,1,0:T(8,128)(2,1)}, bf16[2,128,1024]{2,1,0:T(8,128)(2,1)}, u32[]{:S(2)}, u32[]{:S(2)}) collective-permute-start(bf16[2,128,1024]{2,1,0:T(8,128)(2,1)} %fusion.53), channel_id=1, source_target_pairs={{0,32},{32,0},{64,96},{96,64},{1,33},{33,1},{65,97},{97,65},{2,34}... | collective-permute-start | bytes 1572872 | tf_op jit(solution)/shard_map/ppermute | solution.py:361
  452.0 21.1 %all-to-all-start.4 = ((bf16[32,8,1024]{2,1,0:T(8,128)(2,1)}), bf16[32,8,1024]{2,1,0:T(8,128)(2,1)}, u32[]{:S(2)}, u32[]{:S(2)}) async-start(bf16[32,8,1024]{2,1,0:T(8,128)(2,1)} %convolution_convert_fusion.6), calls=%async_computation.4 | async-start | bytes 1048576 | tf_op jit(solution)/shard_map/all_to_all | solution.py:394
  467.2 70.1 %collective-permute-start.30 = (bf16[1024,512]{1,0:T(8,128)(2,1)}, bf16[1024,512]{1,0:T(8,128)(2,1)}, u32[]{:S(2)}, u32[]{:S(2)}) collective-permute-start(bf16[1024,512]{1,0:T(8,128)(2,1)} %fusion.31), channel_id=1, source_target_pairs={{0,32},{32,0},{64,96},{96,64},{1,33},{33,1},{65,97},{97,65},{2,34}... | collective-permute-start | bytes 3145736 | tf_op jit(solution)/shard_map/ppermute | solution.py:361
  472.9 7.2 %copy-start.55 = (s32[256]{0:T(256)S(1)}, s32[256]{0:T(256)}, u32[]{:S(2)}) copy-start(s32[256]{0:T(256)} %copy-done.54) | copy-start | bytes 3076
  472.9 15.0 %copy-start.56 = (f32[128]{0:T(128)S(1)}, f32[128]{0:T(128)}, u32[]{:S(2)}) copy-start(f32[128]{0:T(128)} %rsqrt.52) | copy-start | bytes 1540
  474.2 15.1 %copy-start.53 = (f32[32,32]{1,0:T(8,128)S(1)}, f32[32,32]{1,0:T(8,128)}, u32[]{:S(2)}) copy-start(f32[32,32]{1,0:T(8,128)} %reshape.983) | copy-start | bytes 12292
  476.6 11.4 %collective-permute-start.20 = (bf16[128,1024]{1,0:T(8,128)(2,1)}, bf16[128,1024]{1,0:T(8,128)(2,1)S(1)}, u32[]{:S(2)}, u32[]{:S(2)}) collective-permute-start(bf16[128,1024]{1,0:T(8,128)(2,1)} %fusion.64), channel_id=1, source_target_pairs={{0,64},{32,96},{64,0},{96,32},{1,65},{33,97},{65,1},{97,33},{2,66}... | collective-permute-start | bytes 786440 | tf_op jit(solution)/shard_map/ppermute | solution.py:357
  476.6 11.4 %collective-permute-start.25 = (bf16[40,1024]{1,0:T(8,128)(2,1)S(1)}, bf16[40,1024]{1,0:T(8,128)(2,1)S(1)}, u32[]{:S(2)}, u32[]{:S(2)}) collective-permute-start(bf16[40,1024]{1,0:T(8,128)(2,1)S(1)} %pad_maximum_fusion.4), channel_id=1, source_target_pairs={{0,0},{4,1},{8,2},{12,3},{16,4},{20,5},{24,6},{28,7},{32,8},{36,9}... | collective-permute-start | bytes 245768 | tf_op jit(solution)/shard_map/ppermute | solution.py:796
  480.7 31.2 %copy-start.32 = (f32[128,1024]{1,0:T(8,128)S(1)}, f32[128,1024]{1,0:T(8,128)}, u32[]{:S(2)}) copy-start(f32[128,1024]{1,0:T(8,128)} %get-tuple-element.129) | copy-start | bytes 1572868
  487.9 10.5 %collective-permute-start.26 = (bf16[40,1024]{1,0:T(8,128)(2,1)S(1)}, bf16[40,1024]{1,0:T(8,128)(2,1)S(1)}, u32[]{:S(2)}, u32[]{:S(2)}) collective-permute-start(bf16[40,1024]{1,0:T(8,128)(2,1)S(1)} %collective-permute-done.25), channel_id=1, source_target_pairs={{0,64},{32,96},{64,0},{96,32},{1,65},{33,97},{65,1},{97,33},{2,66}... | collective-permute-start | bytes 245768 | tf_op jit(solution)/shard_map/ppermute | solution.py:357
  490.1 17.1 %all-to-all-start.2 = ((f32[32,8,128]{2,1,0:T(8,128)}), f32[32,8,128]{2,1,0:T(8,128)}, u32[]{:S(2)}, u32[]{:S(2)}) async-start(f32[32,8,128]{2,1,0:T(8,128)} %broadcast_in_dim.5), calls=%async_computation.2 | async-start | bytes 262144 | tf_op jit(solution)/shard_map/all_to_all | solution.py:784
  499.1 14.8 %collective-permute-start.27 = (bf16[2,40,1024]{2,1,0:T(8,128)(2,1)}, bf16[2,40,1024]{2,1,0:T(8,128)(2,1)}, u32[]{:S(2)}, u32[]{:S(2)}) collective-permute-start(bf16[2,40,1024]{2,1,0:T(8,128)(2,1)} %maximum_select_fusion.14), channel_id=1, source_target_pairs={{0,32},{32,0},{64,96},{96,64},{1,33},{33,1},{65,97},{97,65},{2,34}... | collective-permute-start | bytes 491528 | tf_op jit(solution)/shard_map/ppermute | solution.py:361
  507.2 20.6 %all-to-all-start.3 = ((bf16[32,32,512]{2,1,0:T(8,128)(2,1)}), bf16[32,32,512]{2,1,0:T(8,128)(2,1)}, u32[]{:S(2)}, u32[]{:S(2)}) async-start(bf16[32,32,512]{2,1,0:T(8,128)(2,1)} %convolution_convert_fusion.3), calls=%async_computation.3 | async-start | bytes 2097152 | tf_op jit(solution)/shard_map/all_to_all | solution.py:394
  515.9 2.6 collective-permute-start.21
  518.5 9.3 %collective-permute-start.22 = (f32[8,128]{1,0:T(8,128)S(1)}, f32[8,128]{1,0:T(8,128)S(1)}, u32[]{:S(2)}, u32[]{:S(2)}) collective-permute-start(f32[8,128]{1,0:T(8,128)S(1)} %add.266), channel_id=1, source_target_pairs={{0,32},{32,0},{64,96},{96,64},{1,33},{33,1},{65,97},{97,65},{2,34}... | collective-permute-start | bytes 12296 | tf_op jit(solution)/shard_map/ppermute | solution.py:361
  529.2 2.8 collective-permute-start.23
  532.0 12.5 %collective-permute-start.24 = (bf16[2,32,512]{2,1,0:T(8,128)(2,1)S(1)}, bf16[2,32,512]{2,1,0:T(8,128)(2,1)S(1)}, u32[]{:S(2)}, u32[]{:S(2)}) collective-permute-start(bf16[2,32,512]{2,1,0:T(8,128)(2,1)S(1)} %maximum_select_fusion.20), channel_id=1, source_target_pairs={{0,32},{32,0},{64,96},{96,64},{1,33},{33,1},{65,97},{97,65},{2,34}... | collective-permute-start | bytes 196616 | tf_op jit(solution)/shard_map/ppermute | solution.py:361
  540.5 22.9 %all-to-all-start.8 = ((bf16[32,32,512]{2,1,0:T(8,128)(2,1)}), bf16[32,32,512]{2,1,0:T(8,128)(2,1)S(1)}, u32[]{:S(2)}, u32[]{:S(2)}) async-start(bf16[32,32,512]{2,1,0:T(8,128)(2,1)} %bitcast.178), calls=%async_computation.8 | async-start | bytes 2097152 | tf_op jit(solution)/shard_map/all_to_all | solution.py:394
  563.6 2.8 collective-permute-start.31
  566.4 3.1 collective-permute-start.32
  (48 other events, 117.8 us)
